TPU v7x, 128 devices: a whole 4x4x4 slice. The times are simulated.
128 devices in a mesh: ep: 64 (over x_lo, z, y, core), tp: 2 (over x_hi).
Axes of the slice: x: 4 (x_hi: 2, x_lo: 2; x = x_hi * 2 + x_lo), y: 4, z: 4, core: 2. Of those that a mesh axis runs over, the one named last changes fastest.
Arguments:
- tokens: bfloat16 [8192, 2048], P('ep'), may hold values from -6 to 6
- expert_ids: int32 [8192, 8], P('ep'), may hold values from 0 to 127, all different within a row; in each aligned block of 128 rows (0 to 127, 128 to 255, ...) at most 12 rows name the same one
- combine: float32 [8192, 8], P('ep'), may hold values from 0.05 to 0.5
- cotangent: bfloat16 [8192, 2048], P('ep'), may hold values from -6 to 6
- old_layout: int32 [128], replicated, may hold values from 0 to 127, each once
- pair_moves: int32 [64], replicated, may hold values from 0 to 1, as said below
- gate_w: bfloat16 [128, 2048, 768], P('ep', None, 'tp'), may hold values from -0.125 to 0.125
- up_w: bfloat16 [128, 2048, 768], P('ep', None, 'tp'), may hold values from -0.125 to 0.125
- down_w: bfloat16 [128, 768, 2048], P('ep', 'tp'), may hold values from -0.21875 to 0.21875
Outputs:
- mixed: bfloat16 [8192, 2048], P('ep', 'tp')
- d_tokens: bfloat16 [8192, 2048], P('ep', 'tp')
- d_combine: float32 [8192, 8], P('ep')
- grad_gate: bfloat16 [128, 2048, 768], P('ep', None, 'tp')
- grad_up: bfloat16 [128, 2048, 768], P('ep', None, 'tp')
- grad_down: bfloat16 [128, 768, 2048], P('ep', 'tp')
Inputs may be any that keep to these rules, and one draw needn't show every extreme that they name: `expert_ids`: among the 128 tokens of one ep index no expert is named more than 12 times, a bound that some block reaches. `old_layout`: A permutation of the experts. pair_moves[q] = pair_moves[q + 32]; at least one pair moves.
All inputs are finite; a program needn't handle non-finite values.
Results may differ from a plain program's by a relative error of at most 0.008.
Values may be sent and summed in bfloat16 or wider, within the bound.
A program may use at most 192 MiB of HBM per device.

v0:
```python
import jax
import jax.numpy as jnp
from jax import lax
from jax.sharding import PartitionSpec as P


def from_partner(value, axis, distance):
    mask = 2**distance
    pairs = [(source, source ^ mask) for source in range(lax.axis_size(axis))]
    return lax.ppermute(value, axis, pairs)


def body(tokens, expert_ids, combine, cotangent, old_layout, pair_moves, gate_w, up_w, down_w):
    ep_count = lax.axis_size("ep")
    tp_count = lax.axis_size("tp")
    tok_count, top_k = expert_ids.shape
    expert_count = old_layout.shape[0]
    per_device = gate_w.shape[0]
    model_width = tokens.shape[1]
    share_width = model_width // tp_count
    capacity = 3 * tok_count * top_k // (2 * expert_count)
    pair_count = ep_count // 2
    swap_bit = ep_count.bit_length() - 2
    my_index = lax.axis_index("ep")
    my_share = lax.axis_index("tp")
    my_move = pair_moves[my_index] == 1
    slot_ids = jnp.arange(expert_count, dtype=jnp.int32)
    slot_device = slot_ids // per_device
    slot_local = slot_ids % per_device
    moved = (slot_local == per_device - 1) & (pair_moves[slot_device] == 1)
    source_slot = jnp.where(
        moved, (slot_device + pair_count) % ep_count * per_device + slot_local, slot_ids
    )
    new_layout = jnp.sum(
        jnp.where(source_slot[:, None] == slot_ids[None, :], old_layout[None, :], 0), axis=1
    )
    w_gate, w_up, w_down = (gate_w, up_w, down_w)
    arrived = from_partner(
        (gate_w[per_device - 1], up_w[per_device - 1], down_w[per_device - 1]), "ep", swap_bit
    )
    w_gate = jnp.concatenate(
        [gate_w[:-1], jnp.where(my_move, arrived[0], gate_w[-1])[None]], axis=0
    )
    w_up = jnp.concatenate([up_w[:-1], jnp.where(my_move, arrived[1], up_w[-1])[None]], axis=0)
    w_down = jnp.concatenate(
        [down_w[:-1], jnp.where(my_move, arrived[2], down_w[-1])[None]], axis=0
    )
    slot_of = jnp.sum(
        jnp.where(new_layout[None, :] == slot_ids[:, None], slot_ids[None, :], 0), axis=1
    )
    flat_ids = expert_ids.reshape(-1)
    onehot = (flat_ids[:, None] == slot_ids[None, :]).astype(jnp.int32)
    before = jnp.cumsum(onehot, axis=0) - onehot
    position = jnp.sum(before * onehot, axis=1)
    target_slot = jnp.sum(onehot * slot_of[None, :], axis=1)
    target_device = target_slot // per_device
    target_local = target_slot % per_device
    row_index = target_local * (ep_count * capacity) + target_device * capacity + position
    rows_total = expert_count * capacity
    matches = jnp.arange(rows_total, dtype=jnp.int32)[:, None] == row_index[None, :]
    select = jnp.sum(
        matches.reshape(rows_total, tok_count, top_k).astype(jnp.int32), axis=2
    ).astype(jnp.bfloat16)
    row_weight = jnp.sum(jnp.where(matches, combine.reshape(-1)[None, :], 0.0), axis=1)

    def dispatch(source, scaling):
        picked = jnp.dot(select, source, preferred_element_type=jnp.float32)
        if scaling is not None:
            picked = picked * scaling[:, None]
        buffer = picked.astype(jnp.bfloat16).reshape(per_device, ep_count * capacity, model_width)
        return lax.all_to_all(buffer, "ep", split_axis=1, concat_axis=1, tiled=True)

    def send_back(partial_value):
        shares = lax.psum_scatter(partial_value, "tp", scatter_dimension=2, tiled=True).astype(
            jnp.bfloat16
        )
        returned = lax.all_to_all(shares, "ep", split_axis=1, concat_axis=1, tiled=True)
        return returned.reshape(rows_total, share_width)[row_index].reshape(
            tok_count, top_k, share_width
        )

    rows_in = dispatch(tokens, None)
    gate = jnp.einsum("erd,edf->erf", rows_in, w_gate, preferred_element_type=jnp.float32)
    upper = jnp.einsum("erd,edf->erf", rows_in, w_up, preferred_element_type=jnp.float32)
    sigma = jax.nn.sigmoid(gate)
    active = gate * sigma
    hidden = (active * upper).astype(jnp.bfloat16)
    out_part = jnp.einsum("erf,efd->erd", hidden, w_down, preferred_element_type=jnp.float32)
    out_rows = send_back(out_part).astype(jnp.float32)
    mixed = jnp.einsum("tk,tkd->td", combine, out_rows).astype(jnp.bfloat16)
    cot_share = lax.dynamic_slice_in_dim(cotangent, my_share * share_width, share_width, 1).astype(
        jnp.float32
    )
    combine_part = jnp.einsum("td,tkd->tk", cot_share, out_rows)
    d_combine = lax.psum(combine_part, "tp")
    rows_grad = dispatch(cotangent, row_weight)
    d_hidden = jnp.einsum("erd,efd->erf", rows_grad, w_down, preferred_element_type=jnp.float32)
    d_gate = (d_hidden * upper * sigma * (1.0 + gate * (1.0 - sigma))).astype(jnp.bfloat16)
    d_up = (d_hidden * active).astype(jnp.bfloat16)
    back_part = jnp.einsum(
        "erf,edf->erd", d_gate, w_gate, preferred_element_type=jnp.float32
    ) + jnp.einsum("erf,edf->erd", d_up, w_up, preferred_element_type=jnp.float32)
    back_rows = send_back(back_part)
    d_tokens = jnp.sum(back_rows.astype(jnp.float32), axis=1).astype(jnp.bfloat16)
    grad_gate = jnp.einsum(
        "erd,erf->edf", rows_in, d_gate, preferred_element_type=jnp.float32
    ).astype(jnp.bfloat16)
    grad_up = jnp.einsum("erd,erf->edf", rows_in, d_up, preferred_element_type=jnp.float32).astype(
        jnp.bfloat16
    )
    grad_down = jnp.einsum(
        "erf,erd->efd", hidden, rows_grad, preferred_element_type=jnp.float32
    ).astype(jnp.bfloat16)
    return (mixed, d_tokens, d_combine, grad_gate, grad_up, grad_down)


def solution(mesh):
    return jax.shard_map(
        body,
        mesh=mesh,
        in_specs=(
            P("ep", None),
            P("ep", None),
            P("ep", None),
            P("ep", None),
            P(),
            P(),
            P("ep", None, "tp"),
            P("ep", None, "tp"),
            P("ep", "tp", None),
        ),
        out_specs=(
            P("ep", "tp"),
            P("ep", "tp"),
            P("ep", None),
            P("ep", None, "tp"),
            P("ep", None, "tp"),
            P("ep", "tp", None),
        ),
        check_vma=False,
    )
```

profile of v0, /device:TPU:0, one launch (start us, length us, event | category | flops | bytes accessed | tf_op | source)
XLA Modules:
  0.0 802.9 jit_solution(15792823822360556557)
XLA Ops:
  8.2 1.6 gather_fusion
  12.2 8.0 convert_reduce_fusion
  20.2 1.8 convolution_convert_fusion
  22.0 18.8 %copy.72 = bf16[2,768,2048]{2,0,1:T(2,128)(2,1)} copy(bf16[2,768,2048]{2,1,0:T(8,128)(2,1)S(1)} %bitcast.68) | data formatting | bytes 12582912 | tf_op jit(solution)/shard_map/reshape | solution.py:70
  40.8 10.6 %all-to-all-start = ((bf16[2,768,2048]{2,0,1:T(2,128)(2,1)}), bf16[2,768,2048]{2,0,1:T(2,128)(2,1)}, u32[]{:S(2)}, u32[]{:S(2)}) async-start(bf16[2,768,2048]{2,0,1:T(2,128)(2,1)} %copy.72), calls=%async_computation | async-start | bytes 12582912 | tf_op jit(solution)/shard_map/all_to_all | solution.py:71
  52.3 1.8 multiply_convert_fusion
  54.1 18.8 %copy.78 = bf16[2,768,2048]{2,0,1:T(2,128)(2,1)} copy(bf16[2,768,2048]{2,1,0:T(8,128)(2,1)S(1)} %bitcast.67) | data formatting | bytes 12582912 | tf_op jit(solution)/shard_map/reshape | solution.py:70
  72.9 53.3 %all-to-all-done = bf16[2,768,2048]{2,0,1:T(2,128)(2,1)} async-done(((bf16[2,768,2048]{2,0,1:T(2,128)(2,1)}), bf16[2,768,2048]{2,0,1:T(2,128)(2,1)}, u32[]{:S(2)}, u32[]{:S(2)}) %all-to-all-start) | async-done | bytes 6291488 | tf_op jit(solution)/shard_map/all_to_all | solution.py:71
  126.2 18.0 %all-to-all-start.2 = ((bf16[2,768,2048]{2,0,1:T(2,128)(2,1)}), bf16[2,768,2048]{2,0,1:T(2,128)(2,1)}, u32[]{:S(2)}, u32[]{:S(2)}) async-start(bf16[2,768,2048]{2,0,1:T(2,128)(2,1)} %copy.78), calls=%async_computation.3 | async-start | bytes 12582912 | tf_op jit(solution)/shard_map/all_to_all | solution.py:71
  144.3 4.0 fusion.55
  148.2 1.6 collective-permute-start
  149.8 2.0 fusion.56
  152.2 2.0 fusion.54
  154.3 2.0 collective-permute-start.2
  157.5 95.7 %collective-permute-done = bf16[2048,384]{1,0:T(8,128)(2,1)S(1)} collective-permute-done((bf16[2048,384]{1,0:T(8,128)(2,1)}, bf16[2048,384]{1,0:T(8,128)(2,1)S(1)}, u32[]{:S(2)}, u32[]{:S(2)}) %collective-permute-start) | collective-permute-done | bytes 1572896 | tf_op jit(solution)/shard_map/ppermute | solution.py:10
  253.2 1.1 copy-done.12
  254.3 2.2 select_bitcast_fusion.2
  256.5 30.4 %collective-permute-done.1 = bf16[2048,384]{1,0:T(8,128)(2,1)} collective-permute-done((bf16[2048,384]{1,0:T(8,128)(2,1)}, bf16[2048,384]{1,0:T(8,128)(2,1)}, u32[]{:S(2)}, u32[]{:S(2)}) %collective-permute-start.1) | collective-permute-done | bytes 1572896 | tf_op jit(solution)/shard_map/ppermute | solution.py:10
  287.0 2.8 select_bitcast_fusion.1
  289.8 30.4 %collective-permute-done.2 = bf16[384,2048]{1,0:T(8,128)(2,1)} collective-permute-done((bf16[384,2048]{1,0:T(8,128)(2,1)}, bf16[384,2048]{1,0:T(8,128)(2,1)}, u32[]{:S(2)}, u32[]{:S(2)}) %collective-permute-start.2) | collective-permute-done | bytes 1572896 | tf_op jit(solution)/shard_map/ppermute | solution.py:10
  320.1 2.8 select_bitcast_fusion
  322.9 16.2 %copy.82 = bf16[2,768,2048]{1,2,0:T(8,128)(2,1)} copy(bf16[2,768,2048]{2,0,1:T(2,128)(2,1)} %all-to-all-done) | data formatting | bytes 12582912 | tf_op jit(solution)/shard_map/all_to_all | solution.py:71
  339.1 8.5 %fusion.14 = f32[2,768,384]{2,1,0:T(8,128)} fusion(bf16[2,768,2048]{1,2,0:T(8,128)(2,1)} %copy.82, bf16[1,2048,384]{2,1,0:T(8,128)(2,1)} %select_bitcast_fusion.1, bf16[1,2048,384]{2,1,0:T(8,128)(2,1)} %get-tuple-element.15), kind=kOutput, calls=%fused_computation.32 | convolution fusion | flops 2417491968 | bytes 11796480 | tf_op jit(solution)/shard_map/erd,edf->erf/dot_general | solution.py:84
  347.6 9.2 %fusion.2 = f32[2,768,384]{2,1,0:T(8,128)} fusion(bf16[2,768,2048]{2,0,1:T(2,128)(2,1)} %all-to-all-done.2, bf16[1,384,2048]{2,1,0:T(8,128)(2,1)} %select_bitcast_fusion, bf16[1,384,2048]{2,1,0:T(8,128)(2,1)} %get-tuple-element.11), kind=kOutput, calls=%fused_computation.11 | convolution fusion | flops 2417491968 | bytes 11796480 | tf_op jit(solution)/shard_map/erd,efd->erf/dot_general | solution.py:97
  356.8 7.6 multiply_convert_fusion.2
  364.4 5.3 fusion.13
  369.8 7.6 convolution_add_fusion
  377.5 1.3 copy-done.7
  379.2 7.8 fusion.12
  387.0 147.7 %reduce-scatter.5.cloned.1.call-done = f32[2,768,1024]{2,1,0:T(8,128)} async-done(((f32[2,768,2048]{2,1,0:T(8,128)}), f32[2,768,1024]{2,1,0:T(8,128)}) %reduce-scatter.5.cloned.1.call-update) | async-done | bytes 6291472 | tf_op jit(solution)/shard_map/reduce_scatter | solution.py:74
  534.7 3.3 convert_element_type.61
  538.0 4.9 copy.80
  542.9 8.3 %all-to-all-start.3 = ((bf16[2,768,1024]{2,0,1:T(2,128)(2,1)}), bf16[2,768,1024]{2,0,1:T(2,128)(2,1)}, u32[]{:S(2)}, u32[]{:S(2)}) async-start(bf16[2,768,1024]{2,0,1:T(2,128)(2,1)} %copy.80), calls=%async_computation.5 | async-start | bytes 6291456 | tf_op jit(solution)/shard_map/all_to_all | solution.py:77
  551.2 167.7 %reduce-scatter.3.cloned.1.call-done = f32[2,768,1024]{2,1,0:T(8,128)} async-done(((f32[2,768,2048]{2,1,0:T(8,128)}), f32[2,768,1024]{2,1,0:T(8,128)}) %reduce-scatter.3.cloned.1.call-update) | async-done | bytes 6291472 | tf_op jit(solution)/shard_map/reduce_scatter | solution.py:74
  718.9 3.3 convert_element_type.56
  722.1 4.9 copy.75
  727.1 8.2 %all-to-all-start.1 = ((bf16[2,768,1024]{2,0,1:T(2,128)(2,1)}), bf16[2,768,1024]{2,0,1:T(2,128)(2,1)}, u32[]{:S(2)}, u32[]{:S(2)}) async-start(bf16[2,768,1024]{2,0,1:T(2,128)(2,1)} %copy.75), calls=%async_computation.2 | async-start | bytes 6291456 | tf_op jit(solution)/shard_map/all_to_all | solution.py:77
  735.6 8.3 %convolution_convert_fusion.2 = bf16[2,2048,384]{2,1,0:T(8,128)(2,1)} fusion(bf16[2,768,2048]{1,2,0:T(8,128)(2,1)} %copy.82, bf16[2,768,384]{2,1,0:T(8,128)(2,1)} %get-tuple-element.8), kind=kOutput, calls=%fused_computation.16 | convolution fusion | flops 2417491968 | bytes 10616832 | tf_op jit(solution)/shard_map/erd,erf->edf/dot_general | solution.py:105
  743.9 4.8 convolution_convert_fusion.1
  748.7 9.1 %fusion.4 = bf16[2,384,2048]{2,1,0:T(8,128)(2,1)} fusion(bf16[2,768,384]{2,1,0:T(8,128)(2,1)S(1)} %copy-done.14, bf16[2,768,2048]{2,0,1:T(2,128)(2,1)} %all-to-all-done.2), kind=kOutput, calls=%fused_computation.14 | convolution fusion | flops 2417491968 | bytes 10616832 | tf_op jit(solution)/shard_map/erf,erd->efd/dot_general | solution.py:111
  757.9 4.5 copy.81
  762.4 7.5 gather_fusion.2
  770.0 2.1 bitcast_reduce_fusion
  772.1 2.0 all-to-all-done.1
  774.1 4.5 copy.76
  778.6 7.3 gather_fusion.1
  785.9 1.2 fusion.8
  788.6 7.0 psum.7
  (77 shorter events, 7.5 us)
Async XLA Ops:
  7.2 45.1 %copy-start = (bf16[128,2048]{1,0:T(8,128)(2,1)S(1)}, bf16[128,2048]{1,0:T(8,128)(2,1)}, u32[]{:S(2)}) copy-start(bf16[128,2048]{1,0:T(8,128)(2,1)} %param.12) | copy-start | bytes 1572868
  8.2 12.0 %copy-start.15 = (bf16[128,2048]{1,0:T(8,128)(2,1)S(1)}, bf16[128,2048]{1,0:T(8,128)(2,1)}, u32[]{:S(2)}) copy-start(bf16[128,2048]{1,0:T(8,128)(2,1)} %param.9) | copy-start | bytes 1572868
  40.8 10.6 %copy-start.16 = (f32[128,8]{0,1:T(8,128)S(1)}, f32[128,8]{0,1:T(8,128)}, u32[]{:S(2)}) copy-start(f32[128,8]{0,1:T(8,128)} %param.11) | copy-start | bytes 12292
  40.8 85.4 %all-to-all-start = ((bf16[2,768,2048]{2,0,1:T(2,128)(2,1)}), bf16[2,768,2048]{2,0,1:T(2,128)(2,1)}, u32[]{:S(2)}, u32[]{:S(2)}) async-start(bf16[2,768,2048]{2,0,1:T(2,128)(2,1)} %copy.72), calls=%async_computation | async-start | bytes 12582912 | tf_op jit(solution)/shard_map/all_to_all | solution.py:71
  126.2 221.4 %all-to-all-start.2 = ((bf16[2,768,2048]{2,0,1:T(2,128)(2,1)}), bf16[2,768,2048]{2,0,1:T(2,128)(2,1)}, u32[]{:S(2)}, u32[]{:S(2)}) async-start(bf16[2,768,2048]{2,0,1:T(2,128)(2,1)} %copy.78), calls=%async_computation.3 | async-start | bytes 12582912 | tf_op jit(solution)/shard_map/all_to_all | solution.py:71
  144.2 390.5 %reduce-scatter.5.cloned.1.call-start = ((), (), s32[]{:S(2)}) async-start(), calls=%async_computation.7 | async-start | bytes 18874368 | tf_op jit(solution)/shard_map/reduce_scatter | solution.py:74
  144.3 5.6 copy-start.2
  148.2 4.0 copy-start.4
  148.2 104.9 %collective-permute-start = (bf16[2048,384]{1,0:T(8,128)(2,1)}, bf16[2048,384]{1,0:T(8,128)(2,1)S(1)}, u32[]{:S(2)}, u32[]{:S(2)}) collective-permute-start(bf16[2048,384]{1,0:T(8,128)(2,1)} %get-tuple-element.14), channel_id=1, source_target_pairs={{0,64},{2,66},{4,68},{6,70},{8,72},{10,74},{12,76},{14,78},{16,80}... | collective-permute-start | bytes 4718600 | tf_op jit(solution)/shard_map/ppermute | solution.py:10
  151.8 4.4 copy-start.1
  151.8 135.2 %collective-permute-start.1 = (bf16[2048,384]{1,0:T(8,128)(2,1)}, bf16[2048,384]{1,0:T(8,128)(2,1)}, u32[]{:S(2)}, u32[]{:S(2)}) collective-permute-start(bf16[2048,384]{1,0:T(8,128)(2,1)} %get-tuple-element.16), channel_id=1, source_target_pairs={{0,64},{2,66},{4,68},{6,70},{8,72},{10,74},{12,76},{14,78},{16,80}... | collective-permute-start | bytes 4718600 | tf_op jit(solution)/shard_map/ppermute | solution.py:10
  154.3 165.8 %collective-permute-start.2 = (bf16[384,2048]{1,0:T(8,128)(2,1)}, bf16[384,2048]{1,0:T(8,128)(2,1)}, u32[]{:S(2)}, u32[]{:S(2)}) collective-permute-start(bf16[384,2048]{1,0:T(8,128)(2,1)} %get-tuple-element.12), channel_id=1, source_target_pairs={{0,64},{2,66},{4,68},{6,70},{8,72},{10,74},{12,76},{14,78},{16,80}... | collective-permute-start | bytes 4718600 | tf_op jit(solution)/shard_map/ppermute | solution.py:10
  253.2 1.1 copy-start.12
  254.3 32.7 %copy-start.3 = (bf16[2,2048,384]{2,1,0:T(8,128)(2,1)S(1)}, bf16[2,2048,384]{2,1,0:T(8,128)(2,1)}, u32[]{:S(2)}) copy-start(bf16[2,2048,384]{2,1,0:T(8,128)(2,1)} %param.16) | copy-start | bytes 9437188
  256.5 63.6 %copy-start.5 = (bf16[2,384,2048]{2,1,0:T(8,128)(2,1)S(1)}, bf16[2,384,2048]{2,1,0:T(8,128)(2,1)}, u32[]{:S(2)}) copy-start(bf16[2,384,2048]{2,1,0:T(8,128)(2,1)} %param.17) | copy-start | bytes 9437188
  347.6 9.2 %copy-start.6 = (bf16[1,2048,384]{2,1,0:T(8,128)(2,1)S(1)}, bf16[1,2048,384]{2,1,0:T(8,128)(2,1)}, u32[]{:S(2)}) copy-start(bf16[1,2048,384]{2,1,0:T(8,128)(2,1)} %get-tuple-element.13) | copy-start | bytes 4718596
  347.6 9.2 %copy-start.8 = (bf16[2,768,2048]{1,2,0:T(8,128)(2,1)S(1)}, bf16[2,768,2048]{1,2,0:T(8,128)(2,1)}, u32[]{:S(2)}) copy-start(bf16[2,768,2048]{1,2,0:T(8,128)(2,1)} %copy.82) | copy-start | bytes 18874372
  356.8 7.6 copy-start.9
  364.4 5.3 copy-start.10
  377.4 1.4 copy-start.7
  377.4 1.7 copy-start.13
  377.4 341.4 %reduce-scatter.3.cloned.1.call-start = ((), (), s32[]{:S(2)}) async-start(), calls=%async_computation.6 | async-start | bytes 18874368 | tf_op jit(solution)/shard_map/reduce_scatter | solution.py:74
  542.9 184.2 %all-to-all-start.3 = ((bf16[2,768,1024]{2,0,1:T(2,128)(2,1)}), bf16[2,768,1024]{2,0,1:T(2,128)(2,1)}, u32[]{:S(2)}, u32[]{:S(2)}) async-start(bf16[2,768,1024]{2,0,1:T(2,128)(2,1)} %copy.80), calls=%async_computation.5 | async-start | bytes 6291456 | tf_op jit(solution)/shard_map/all_to_all | solution.py:77
  727.1 16.9 %slice-start = ((s8[6291456]{0:T(1024)(128)(4,1)}), s8[2097152]{0:T(1024)(128)(4,1)S(1)}, s32[]{:S(2)}) async-start(s8[6291456]{0:T(1024)(128)(4,1)} %bitcast.69), calls=%async_computation.8 | async-start | bytes 4194304
  727.1 47.0 %all-to-all-start.1 = ((bf16[2,768,1024]{2,0,1:T(2,128)(2,1)}), bf16[2,768,1024]{2,0,1:T(2,128)(2,1)}, u32[]{:S(2)}, u32[]{:S(2)}) async-start(bf16[2,768,1024]{2,0,1:T(2,128)(2,1)} %copy.75), calls=%async_computation.2 | async-start | bytes 6291456 | tf_op jit(solution)/shard_map/all_to_all | solution.py:77
  735.6 8.4 %slice-start.1 = ((s8[6291456]{0:T(1024)(128)(4,1)}), s8[4194304]{0:T(1024)(128)(4,1)S(1)}, s32[]{:S(2)}) async-start(s8[6291456]{0:T(1024)(128)(4,1)} %bitcast.69), calls=%async_computation.9 | async-start | bytes 8388608
  735.6 8.4 %copy-start.11 = (bf16[2,768,384]{2,1,0:T(8,128)(2,1)S(1)}, bf16[2,768,384]{2,1,0:T(8,128)(2,1)}, u32[]{:S(2)}) copy-start(bf16[2,768,384]{2,1,0:T(8,128)(2,1)} %copy-done.10) | copy-start | bytes 3538948
  743.9 4.8 copy-start.14
Sparse Core Ops, SparseCore 0:
  377.6 157.0 reduce-scatter.4
  537.1 181.7 reduce-scatter.2
where the time goes:
time: 814 us; the launch traced here: 803 us
  waiting for transfers between devices  527 us (65%)
  local copies, waits for them, and re-layouts  103 us (13%)
  matrix products  73.8 us (9%)
  starting transfers between devices  49.3 us (6%)
  other arithmetic  26.9 us (3%)
  between operations  15.5 us (2%)
    reduce_scatter x2, waiting for transfers between devices, send_back(): lax.psum_scatter(partial_value, 'tp', scatter_dimension=2, tiled=True)  315 us
    ppermute x3, waiting for transfers between devices, from_partner(): return lax.ppermute(value, axis, pairs)  156 us
    all_to_all x2, waiting for transfers between devices, dispatch(): return lax.all_to_all(buffer, 'ep', split_axis=1, concat_axis=1, tiled=True)  53.3 us
    reshape x2, local copies, waits for them, and re-layouts, dispatch(): picked.astype(jnp.bfloat16)  37.5 us
    all_to_all x2, starting transfers between devices, dispatch(): return lax.all_to_all(buffer, 'ep', split_axis=1, concat_axis=1, tiled=True)  28.6 us
    all_to_all x2, starting transfers between devices, send_back(): lax.all_to_all(shares, 'ep', split_axis=1, concat_axis=1, tiled=True)  16.6 us
  transfers between devices with their start and end apart: 9, of which 7 were waited for; matrix products, arithmetic and copies ran while one was open for 15% of the time, Pallas kernels for 0%

commit v1 on v0

v1 whole, which is shorter than its diff:
```python
import jax
import jax.numpy as jnp
from jax import lax
from jax.experimental import pallas as pl
from jax.experimental.pallas import tpu as pltpu
from jax.sharding import Mesh, PartitionSpec as P

MESH = pl.DeviceIdType.MESH
BF, F32 = jnp.bfloat16, jnp.float32
D, FF, CAP, TOK, TOP = 2048, 384, 12, 128, 8
META = 128
WIDE = D + META
BLOCKS = 8
ROWS = BLOCKS * CAP
ALL = BLOCKS * ROWS
HALF = D // 2
LIMIT = 66 * 1024 * 1024 - 4096
EP = ("xlo", "z", "y", "c")
ANY = pl.BlockSpec(memory_space=pl.ANY)
VMEM = pl.BlockSpec(memory_space=pltpu.VMEM)


def position():
    return {name: lax.axis_index(name) for name in ("xlo", "z", "y", "c", "xhi")}


def greet(devices):
    barrier = pltpu.get_barrier_semaphore()
    for device in devices:
        pl.semaphore_signal(barrier, inc=1, device_id=device, device_id_type=MESH)
    pl.semaphore_wait(barrier, len(devices))


def remote(source, target, send, recv, device):
    return pltpu.make_async_remote_copy(
        src_ref=source,
        dst_ref=target,
        send_sem=send,
        recv_sem=recv,
        device_id=device,
        device_id_type=MESH,
    )


def others(axis, me):
    found = []
    for step in range(1, 8):
        j = lax.rem(me + step, 8)
        found.append({axis: j // 2, "c": lax.rem(j, 2)})
    return found


def dispatch_kernel(
    tok_ref, cot_ref, e_tok, e_cot, wg, wu, wd,
    x_out, dy_out, st_tok_out, st_cot_out, wg_out, wu_out, wd_out,
    g_tok, g_cot, sel_tok, sel_cot, st_tok, st_cot, code_tok, code_cot, rowcode, upper,
    ag_send, ag_recv, x_send, x_recv, st_sem, loc_sem, w_send, w_recv,
):
    at = position()
    xlo, y, z, c, xhi = at["xlo"], at["y"], at["z"], at["c"], at["xhi"]
    direct, flipped = {"xlo": 1 - xlo}, {"xlo": 1 - xlo, "xhi": 1 - xhi}
    me_z, me_y = z * 2 + c, y * 2 + c
    greet([direct, flipped] + others("z", me_z) + others("y", me_y))

    paths = ((tok_ref, g_tok, "y", y, 0), (cot_ref, g_cot, "z", z, 1))

    def copies(source, gathered, axis, a, p):
        right, left = {axis: lax.rem(a + 1, 4)}, {axis: lax.rem(a + 3, 4)}
        opposite = lax.rem(a + 2, 4)
        mine, theirs = xlo * 4, (1 - xlo) * 4
        l, r = lax.rem(a + 3, 4), lax.rem(a + 1, 4)
        lo, hi = pl.ds(0, 64), pl.ds(64, 64)
        own = gathered.at[mine + a]
        plan = [
            (source, own, flipped, gathered.at[theirs + a]),
            (source, own, right, gathered.at[mine + l]),
            (source, own, left, gathered.at[mine + r]),
            (gathered.at[theirs + a], gathered.at[theirs + a], right, gathered.at[theirs + l]),
            (gathered.at[theirs + a], gathered.at[theirs + a], left, gathered.at[theirs + r]),
            (gathered.at[mine + l, lo], gathered.at[mine + l, lo], right, gathered.at[mine + opposite, lo]),
            (gathered.at[theirs + l, lo], gathered.at[theirs + l, lo], right, gathered.at[theirs + opposite, lo]),
            (gathered.at[mine + r, hi], gathered.at[mine + r, hi], left, gathered.at[mine + opposite, hi]),
            (gathered.at[theirs + r, hi], gathered.at[theirs + r, hi], left, gathered.at[theirs + opposite, hi]),
        ]
        out = [remote(s, t, ag_send.at[p, i], ag_recv.at[p, i], dev) for i, (s, t, dev, _) in enumerate(plan)]
        come = [remote(s, got, ag_send.at[p, i], ag_recv.at[p, i], dev) for i, (s, _, dev, got) in enumerate(plan)]
        local = pltpu.make_async_copy(source, own, loc_sem.at[p])
        return out, come, local

    tok, cot = copies(*paths[0]), copies(*paths[1])
    for out, _, local in (tok, cot):
        for i in (1, 2, 0):
            out[i].start()
        local.start()
    weights = [
        remote(src.at[1], dst, w_send.at[i], w_recv.at[i], direct)
        for i, (src, dst) in enumerate(((wg, wg_out), (wu, wu_out), (wd, wd_out)))
    ]
    for copy in weights:
        copy.start()

    row = lax.broadcasted_iota(jnp.int32, (ROWS, BLOCKS * TOK), 0)
    col = lax.broadcasted_iota(jnp.int32, (ROWS, BLOCKS * TOK), 1)
    value = jnp.full((ROWS, BLOCKS * TOK), -2, jnp.int32)
    for b in range(BLOCKS):
        inside = (row >= b * CAP) & (row < (b + 1) * CAP) & (col >= b * TOK) & (col < (b + 1) * TOK)
        value = jnp.where(inside, row - b * CAP, value)
    rowcode[...] = value.astype(F32)
    before = lax.broadcasted_iota(jnp.int32, (TOK, TOK), 0) < lax.broadcasted_iota(jnp.int32, (TOK, TOK), 1)
    upper[...] = jnp.where(before, 1.0, 0.0).astype(BF)

    for arrival, starts in ((0, (3, 4)), (1, (5,)), (2, (7,)), (3, (6,)), (4, (8,))):
        for out, come, _ in (tok, cot):
            come[arrival].wait_recv()
            for i in starts:
                out[i].start()
    for out, come, local in (tok, cot):
        for i in (5, 6, 7, 8):
            come[i].wait_recv()
        local.wait()

    for gathered, experts, code in ((g_tok, e_tok, code_tok), (g_cot, e_cot, code_cot)):
        for b in range(BLOCKS):
            ids = gathered[b, :, D:WIDE].astype(F32).T[0:TOP]
            member = jnp.zeros((16, TOK), F32)
            for k in range(TOP):
                member = member + jnp.where(ids[k : k + 1] == experts[...], 1.0, 0.0)
            place = jnp.dot(member.astype(BF), upper[...], preferred_element_type=F32)
            found = jnp.where(member > 0.5, place, -1.0)
            for d in range(8):
                code[d, 0:2, b * TOK : (b + 1) * TOK] = found[2 * d : 2 * d + 2]

    def emit(d, gathered, code, sel, st, width):
        rows = code[d]
        chosen = jnp.concatenate(
            [jnp.where(rowcode[...] == rows[l : l + 1], 1.0, 0.0) for l in range(2)], axis=0
        )
        st[d] = chosen.T.astype(BF)
        pick = chosen.astype(BF)

        def piece(start, size):
            source = gathered[:, :, pl.ds(start, size)].reshape(BLOCKS * TOK, size)
            got = jnp.dot(pick, source, preferred_element_type=F32).astype(BF)
            sel[d, :, :, pl.ds(start, size)] = got.reshape(2, ROWS, size)

        def step(n, carry):
            piece(pl.multiple_of(n * 256, 256), 256)
            return carry

        lax.fori_loop(0, D // 256, step, 0)
        if width > D:
            piece(D, META)

    sides = (
        (0, g_tok, code_tok, sel_tok, st_tok, st_tok_out, x_out, "z", me_z, WIDE),
        (1, g_cot, code_cot, sel_cot, st_cot, st_cot_out, dy_out, "y", me_y, D),
    )

    def exchange(p, j, sel, target, axis, slot):
        return remote(
            sel.at[j], target.at[:, slot], x_send.at[p, j], x_recv.at[p, slot],
            {axis: j // 2, "c": lax.rem(j, 2)},
        )

    def send(i, carry):
        for p, gathered, code, sel, st, st_out, target, axis, me, width in sides:
            d = lax.rem(me + i, 8)
            emit(d, gathered, code, sel, st, width)
            exchange(p, d, sel, target, axis, me).start()
            pltpu.make_async_copy(st.at[d], st_out.at[d], st_sem.at[p, d]).start()
        return carry

    lax.fori_loop(1, 8, send, 0)
    for p, gathered, code, sel, st, st_out, target, axis, me, width in sides:
        emit(me, gathered, code, sel, st, width)
        pltpu.make_async_copy(sel.at[me], target.at[:, me], loc_sem.at[2 + p]).start()
        pltpu.make_async_copy(st.at[me], st_out.at[me], st_sem.at[p, me]).start()

    def finish(i, carry):
        for p, gathered, code, sel, st, st_out, target, axis, me, width in sides:
            j = lax.rem(me + i, 8)
            exchange(p, j, sel, target, axis, j).wait_send()
            exchange(p, j, sel, target, axis, j).wait_recv()
            pltpu.make_async_copy(st.at[j], st_out.at[j], st_sem.at[p, j]).wait()
        return carry

    lax.fori_loop(1, 8, finish, 0)
    for p, gathered, code, sel, st, st_out, target, axis, me, width in sides:
        pltpu.make_async_copy(sel.at[me], target.at[:, me], loc_sem.at[2 + p]).wait()
        pltpu.make_async_copy(st.at[me], st_out.at[me], st_sem.at[p, me]).wait()
    for out, _, _ in (tok, cot):
        for copy in out:
            copy.wait_send()
    for copy in weights:
        copy.wait()


def dispatch(tok, cot, e_tok, e_cot, wg, wu, wd):
    gathered = pltpu.VMEM((BLOCKS, TOK, WIDE), BF)
    choice = pltpu.VMEM((8, BLOCKS * TOK, 2 * ROWS), BF)
    code = pltpu.VMEM((8, 8, BLOCKS * TOK), F32)
    dma = pltpu.SemaphoreType.DMA
    return pl.pallas_call(
        dispatch_kernel,
        name="dispatch",
        out_shape=(
            jax.ShapeDtypeStruct((2, 8, ROWS, WIDE), BF),
            jax.ShapeDtypeStruct((2, 8, ROWS, D), BF),
            jax.ShapeDtypeStruct((8, BLOCKS * TOK, 2 * ROWS), BF),
            jax.ShapeDtypeStruct((8, BLOCKS * TOK, 2 * ROWS), BF),
            jax.ShapeDtypeStruct((D, FF), BF),
            jax.ShapeDtypeStruct((D, FF), BF),
            jax.ShapeDtypeStruct((FF, D), BF),
        ),
        in_specs=[ANY, ANY, VMEM, VMEM, ANY, ANY, ANY],
        out_specs=[ANY] * 7,
        scratch_shapes=[
            gathered, gathered,
            pltpu.VMEM((8, 2, ROWS, WIDE), BF), pltpu.VMEM((8, 2, ROWS, D), BF),
            choice, choice, code, code,
            pltpu.VMEM((ROWS, BLOCKS * TOK), F32), pltpu.VMEM((TOK, TOK), BF),
            dma((2, 9)), dma((2, 9)), dma((2, 8)), dma((2, 8)), dma((2, 8)), dma((4,)), dma((3,)), dma((3,)),
        ],
        compiler_params=pltpu.CompilerParams(
            collective_id=0, has_side_effects=True, vmem_limit_bytes=LIMIT
        ),
    )(tok, cot, e_tok, e_cot, wg, wu, wd)


def expert_kernel(
    facts, x, dy, perm, wg, wu, wd, wg_new, wu_new, wd_new,
    y, dx, gg, gu, gd,
    vg, vu, vd, gate, upper, dh_hi, dh_lo, hid, dgate, dup, hid_c, dgate_c, dup_c, sem,
):
    l = pl.program_id(0)
    moved = facts[0] == 1
    pairs = ((wg, wg_new, vg), (wu, wu_new, vu), (wd, wd_new, vd))

    @pl.when(l == 0)
    def _():
        for i, (old, new, held) in enumerate(pairs):
            pltpu.make_async_copy(old.at[0], held.at[0], sem.at[0, i]).start()
        for i, (old, new, held) in enumerate(pairs):

            @pl.when(moved)
            def _(new=new, held=held, i=i):
                pltpu.make_async_copy(new, held.at[1], sem.at[1, i]).start()

            @pl.when(jnp.logical_not(moved))
            def _(old=old, held=held, i=i):
                pltpu.make_async_copy(old.at[1], held.at[1], sem.at[1, i]).start()

    for i, (old, new, held) in enumerate(pairs):
        pltpu.make_async_copy(old.at[0], held.at[l], sem.at[l, i]).wait()
    expert = jnp.where(l == 0, facts[1], facts[2]).astype(F32)

    def nt(a, b):
        return lax.dot_general(a, b, (((1,), (1,)), ((), ())), preferred_element_type=F32)

    def tn(a, b):
        return lax.dot_general(a, b, (((0,), (0,)), ((), ())), preferred_element_type=F32)

    def nn(a, b):
        return jnp.dot(a, b, preferred_element_type=F32)

    def first(i, carry):
        rows = pl.ds(pl.multiple_of(i * 384, 384), 384)
        own = x[0, rows, 0:D]
        gate[rows] = nn(own, vg[l])
        upper[rows] = nn(own, vu[l])
        dh = nt(dy[0, rows], vd[l])
        high = dh.astype(BF)
        dh_hi[rows] = high
        dh_lo[rows] = (dh - high.astype(F32)).astype(BF)
        return carry

    lax.fori_loop(0, ALL // 384, first, 0)

    def second(i, carry):
        rows = pl.ds(pl.multiple_of(i * 192, 192), 192)
        order = perm[rows]
        dh = nn(order, dh_hi[...]) + nn(order, dh_lo[...])
        g, u = gate[rows], upper[rows]
        sigma = jax.nn.sigmoid(g)
        active = g * sigma
        hidden = active * u
        meta = x[0, rows, D:WIDE].astype(F32)
        lane = lax.broadcasted_iota(jnp.int32, meta.shape, 1)
        named = jnp.where((meta == expert) & (lane < TOP), 1.0, 0.0)
        weight = pltpu.roll(meta, META - 8, 1) + (
            pltpu.roll(meta, META - 16, 1) + pltpu.roll(meta, META - 24, 1)
        )
        w = jnp.sum(named * weight, axis=1, keepdims=True)
        dc = jnp.sum(hidden * dh, axis=1, keepdims=True)
        y[0, rows, D:WIDE] = (named * dc).astype(BF)
        hid[rows] = (hidden * w).astype(BF)
        dh = dh * w
        dgate[rows] = (dh * u * sigma * (1.0 + g * (1.0 - sigma))).astype(BF)
        dup[rows] = (dh * active).astype(BF)
        return carry

    lax.fori_loop(0, ALL // 192, second, 0)

    def third(i, carry):
        rows = pl.ds(pl.multiple_of(i * 192, 192), 192)
        order = perm[rows]
        y[0, rows, 0:D] = nn(hid[rows], vd[l]).astype(BF)
        a = nn(order, dgate[...]).astype(BF)
        b = nn(order, dup[...]).astype(BF)
        hid_c[rows] = nn(order, hid[...]).astype(BF)
        dx[0, rows] = (nt(a, vg[l]) + nt(b, vu[l])).astype(BF)
        return carry

    lax.fori_loop(0, ALL // 192, third, 0)

    def fourth(i, carry):
        cols = pl.ds(pl.multiple_of(i * 512, 512), 512)
        own = x[0, :, cols]
        gg[0, cols] = tn(own, dgate[...]).astype(BF)
        gu[0, cols] = tn(own, dup[...]).astype(BF)
        gd[0, :, cols] = tn(hid_c[...], dy[0, :, cols]).astype(BF)
        return carry

    lax.fori_loop(0, D // 512, fourth, 0)


def experts(facts, x, dy, perm, wg, wu, wd, wg_new, wu_new, wd_new):
    def block(*shape):
        return pl.BlockSpec((1, *shape), lambda l: (l,) + (0,) * len(shape))

    small = pltpu.VMEM((ALL, FF), BF)
    wide = pltpu.VMEM((ALL, FF), F32)
    return pl.pallas_call(
        expert_kernel,
        name="experts",
        grid=(2,),
        out_shape=(
            jax.ShapeDtypeStruct((2, ALL, WIDE), BF),
            jax.ShapeDtypeStruct((2, ALL, D), BF),
            jax.ShapeDtypeStruct((2, D, FF), BF),
            jax.ShapeDtypeStruct((2, D, FF), BF),
            jax.ShapeDtypeStruct((2, FF, D), BF),
        ),
        in_specs=[
            pl.BlockSpec(memory_space=pltpu.SMEM),
            block(ALL, WIDE), block(ALL, D),
            pl.BlockSpec((ALL, ALL), lambda l: (0, 0), pipeline_mode=pl.Buffered(1)),
            ANY, ANY, ANY, ANY, ANY, ANY,
        ],
        out_specs=[block(ALL, WIDE), block(ALL, D), block(D, FF), block(D, FF), block(FF, D)],
        scratch_shapes=[
            pltpu.VMEM((2, D, FF), BF), pltpu.VMEM((2, D, FF), BF), pltpu.VMEM((2, FF, D), BF),
            wide, wide, small, small, small, small, small, small, small, small,
            pltpu.SemaphoreType.DMA((2, 3)),
        ],
        compiler_params=pltpu.CompilerParams(
            dimension_semantics=("arbitrary",), vmem_limit_bytes=LIMIT
        ),
    )(facts, x, dy, perm, wg, wu, wd, wg_new, wu_new, wd_new)


def return_kernel(
    y_ref, dx_ref, st_tok, st_cot,
    mixed, d_tokens, d_combine,
    c_tok, c_cot, s_tok, s_cot, m_tok, m_cot, rx_tok, rx_cot, xs_tok, xs_cot, ra_tok, ra_cot,
    a_send, a_recv, x_send, x_recv, f_send, f_recv, loc_sem,
):
    at = position()
    xlo, y, z, c, xhi = at["xlo"], at["y"], at["z"], at["c"], at["xhi"]
    me_z, me_y = z * 2 + c, y * 2 + c
    flips = ((0, 1), (1, 0), (1, 1))
    near = []
    for fx, ft in flips:
        near.append((1 - xlo if fx else xlo, 1 - xhi if ft else xhi))
    greet([{"xlo": a, "xhi": b} for a, b in near] + others("z", me_z) + others("y", me_y))

    sides = (
        (0, y_ref, c_tok, st_tok, s_tok, m_tok, rx_tok, xs_tok, ra_tok, "z", me_z, "y", y, HALF + META),
        (1, dx_ref, c_cot, st_cot, s_cot, m_cot, rx_cot, xs_cot, ra_cot, "y", me_y, "z", z, HALF),
    )

    def exchange(p, source, held, axis, j, slot):
        return remote(
            source.at[:, j], held.at[slot], a_send.at[p, j], a_recv.at[p, slot],
            {axis: j // 2, "c": lax.rem(j, 2)},
        )

    def send(i, carry):
        for p, source, held, st, s, m, rx, xs, ra, axis, me, other, a, width in sides:
            exchange(p, source, held, axis, lax.rem(me + i, 8), me).start()
        return carry

    lax.fori_loop(1, 8, send, 0)
    for p, source, held, st, s, m, rx, xs, ra, axis, me, other, a, width in sides:
        pltpu.make_async_copy(source.at[:, me], held.at[me], loc_sem.at[p]).start()
        pltpu.make_async_copy(st, s, loc_sem.at[2 + p]).start()

    def spread(p, m, rx, k):
        a, b = near[k]
        return remote(m.at[a, b], rx.at[xlo * 2 + xhi], x_send.at[p, k], x_recv.at[p, k], {"xlo": a, "xhi": b})

    for p, source, held, st, s, m, rx, xs, ra, axis, me, other, a, width in sides:

        def arrive(i, carry):
            exchange(p, source, held, axis, lax.rem(me + i, 8), lax.rem(me + i, 8)).wait_recv()
            return carry

        lax.fori_loop(1, 8, arrive, 0)
        pltpu.make_async_copy(source.at[:, me], held.at[me], loc_sem.at[p]).wait()
        pltpu.make_async_copy(st, s, loc_sem.at[2 + p]).wait()

        def total(start, size):
            acc = jnp.zeros((BLOCKS * TOK, size), F32)
            for d in range(8):
                part = held[d, :, :, pl.ds(start, size)].reshape(2 * ROWS, size)
                acc = acc + jnp.dot(s[d], part, preferred_element_type=F32)
            return acc.astype(BF).reshape(2, 4, TOK, size)

        for t in range(2):

            def step(n, carry):
                got = total(pl.multiple_of(t * HALF + n * 256, 256), 256)
                cols = pl.ds(pl.multiple_of(n * 256, 256), 256)
                for b in range(2):
                    m[b, t, :, :, cols] = got[b]
                return carry

            lax.fori_loop(0, HALF // 256, step, 0)
        if width > HALF:
            got = total(D, META)
            for t in range(2):
                for b in range(2):
                    m[b, t, :, :, HALF:width] = got[b]
        for k in range(3):
            spread(p, m, rx, k).start()

    def fold(p, xs, ra, other, a, k, slot):
        to = lax.rem(a + k, 4)
        return remote(xs.at[to], ra.at[slot], f_send.at[p, k], f_recv.at[p, k], {other: to})

    for p, source, held, st, s, m, rx, xs, ra, axis, me, other, a, width in sides:
        for k in range(3):
            spread(p, m, rx, k).wait_recv()

        def add(i, carry):
            acc = m[xlo, xhi, i].astype(F32)
            for k in range(3):
                acc = acc + rx[near[k][0] * 2 + near[k][1], i].astype(F32)
            xs[i] = acc.astype(BF)
            return carry

        lax.fori_loop(0, 4, add, 0)
        for k in range(1, 4):
            fold(p, xs, ra, other, a, k, a).start()

    for p, source, held, st, s, m, rx, xs, ra, axis, me, other, a, width in sides:
        for k in range(1, 4):
            fold(p, xs, ra, other, a, k, a).wait_recv()
        acc = xs[a].astype(F32)
        for k in range(1, 4):
            acc = acc + ra[lax.rem(a + k, 4)].astype(F32)
        (mixed, d_tokens)[p][...] = acc[:, 0:HALF].astype(BF)
        if width > HALF:
            d_combine[...] = acc[:, HALF : HALF + TOP]
    for p, source, held, st, s, m, rx, xs, ra, axis, me, other, a, width in sides:

        def sent(i, carry):
            exchange(p, source, held, axis, lax.rem(me + i, 8), me).wait_send()
            return carry

        lax.fori_loop(1, 8, sent, 0)
        for k in range(3):
            spread(p, m, rx, k).wait_send()
            fold(p, xs, ra, other, a, k + 1, a).wait_send()


def give_back(y, dx, st_tok, st_cot):
    dma = pltpu.SemaphoreType.DMA
    choice = pltpu.VMEM((8, BLOCKS * TOK, 2 * ROWS), BF)
    wide = HALF + META

    def both(*shape):
        return [pltpu.VMEM((*shape, wide), BF), pltpu.VMEM((*shape, HALF), BF)]

    return pl.pallas_call(
        return_kernel,
        name="give_back",
        out_shape=(
            jax.ShapeDtypeStruct((TOK, HALF), BF),
            jax.ShapeDtypeStruct((TOK, HALF), BF),
            jax.ShapeDtypeStruct((TOK, TOP), F32),
        ),
        in_specs=[ANY] * 4,
        out_specs=[VMEM] * 3,
        scratch_shapes=[
            pltpu.VMEM((8, 2, ROWS, WIDE), BF), pltpu.VMEM((8, 2, ROWS, D), BF),
            choice, choice,
            *both(2, 2, 4, TOK), *both(4, 4, TOK), *both(4, TOK), *both(4, TOK),
            dma((2, 8)), dma((2, 8)), dma((2, 3)), dma((2, 3)), dma((2, 4)), dma((2, 4)), dma((4,)),
        ],
        compiler_params=pltpu.CompilerParams(
            collective_id=1, has_side_effects=True, vmem_limit_bytes=LIMIT
        ),
    )(y, dx, st_tok, st_cot)


def body(tokens, expert_ids, combine, cotangent, old_layout, pair_moves, gate_w, up_w, down_w):
    at = position()
    xlo, y, z, c = at["xlo"], at["y"], at["z"], at["c"]
    slots = jnp.arange(128, dtype=jnp.int32)
    owner, local = slots // 2, slots % 2
    moved = (local == 1) & (pair_moves[owner] == 1)
    source = jnp.where(moved, (owner + 32) % 64 * 2 + local, slots)
    new_layout = jnp.sum(jnp.where(source[:, None] == slots[None, :], old_layout[None, :], 0), axis=1)
    by_place = new_layout.reshape(2, 4, 4, 4)
    plane = lax.dynamic_index_in_dim(by_place, xlo, 0, False)
    at_y = lax.dynamic_index_in_dim(plane, y, 1, False)
    at_z = lax.dynamic_index_in_dim(plane, z, 0, False)
    own = lax.dynamic_slice(at_z.reshape(16), ((y * 2 + c) * 2,), (2,))
    device = ((xlo * 4 + z) * 4 + y) * 2 + c
    flag = lax.dynamic_slice(pair_moves, (device,), (1,))
    facts = jnp.concatenate([flag, own])
    e_tok = jnp.broadcast_to(at_y.reshape(16, 1), (16, TOK)).astype(F32)
    e_cot = jnp.broadcast_to(at_z.reshape(16, 1), (16, TOK)).astype(F32)

    high = lax.reduce_precision(combine, 8, 7)
    middle = lax.reduce_precision(combine - high, 8, 7)
    low = lax.reduce_precision(combine - high - middle, 8, 7)
    meta = jnp.concatenate(
        [expert_ids.astype(BF), high.astype(BF), middle.astype(BF), low.astype(BF), jnp.zeros((TOK, META - 32), BF)],
        axis=1,
    )
    tok = jnp.concatenate([tokens, meta], axis=1)
    cot = jnp.concatenate([cotangent, meta], axis=1)
    x, dy, st_tok, st_cot, wg_new, wu_new, wd_new = dispatch(tok, cot, e_tok, e_cot, gate_w, up_w, down_w)

    r = jnp.arange(ALL, dtype=jnp.int32)
    there = (r // CAP % 4 * 2 + r // ROWS % 2) * ROWS + (r // (4 * CAP) % 2 * 4 + r // (2 * ROWS)) * CAP + r % CAP
    perm = (there[:, None] == r[None, :]).astype(BF)
    y_rows, dx_rows, gg, gu, gd = experts(
        facts, x.reshape(2, ALL, WIDE), dy.reshape(2, ALL, D), perm,
        gate_w, up_w, down_w, wg_new, wu_new, wd_new,
    )
    mixed, d_tokens, d_combine = give_back(
        y_rows.reshape(2, 8, ROWS, WIDE), dx_rows.reshape(2, 8, ROWS, D), st_tok, st_cot
    )
    return mixed, d_tokens, d_combine, gg, gu, gd


def solution(mesh):
    fine = Mesh(mesh.devices.reshape(2, 4, 4, 2, 2), (*EP, "xhi"))
    return jax.shard_map(
        body,
        mesh=fine,
        in_specs=(
            P(EP, None), P(EP, None), P(EP, None), P(EP, None), P(), P(),
            P(EP, None, "xhi"), P(EP, None, "xhi"), P(EP, "xhi", None),
        ),
        out_specs=(
            P(EP, "xhi"), P(EP, "xhi"), P(EP, None),
            P(EP, None, "xhi"), P(EP, None, "xhi"), P(EP, "xhi", None),
        ),
        check_vma=False,
    )
```

time: 814 us -> 402 us (0.49)
  waiting for transfers between devices: 527 us -> 0 us
  Pallas kernels: 0 us -> 377 us
  local copies, waits for them, and re-layouts: 103 us -> 14.8 us
  matrix products: 73.8 us -> 0 us
  starting transfers between devices: 49.3 us -> 0 us
  other arithmetic: 26.9 us -> 4.21 us
  between operations: 15.5 us -> 0.72 us
    pallas_call x0 -> x3, Pallas kernels: none -> 377 us  [the longest x1 178 us: give_back(): pl.pallas_call(return_kernel, name='give_back', out_shape=(jax.ShapeDtype...]
    reduce_scatter x2 -> x0, waiting for transfers between devices: 315 us -> none  [send_back(): lax.psum_scatter(partial_value, 'tp', scatter_dimension=2, tiled=True)]
    ppermute x3 -> x0, waiting for transfers between devices: 156 us -> none  [from_partner(): return lax.ppermute(value, axis, pairs)]
    dot_general x13 -> x0, matrix products: 73.8 us -> none  [the longest x1 9.2 us: body(): jnp.einsum('erd,efd->erf', rows_grad, w_down, preferred_element_type=jnp....]
    all_to_all x4 -> x0, waiting for transfers between devices: 55.3 us -> none  [the longest x2 53.3 us: dispatch(): return lax.all_to_all(buffer, 'ep', split_axis=1, concat_axis=1, tiled=True)]
    all_to_all x4 -> x0, starting transfers between devices: 45.2 us -> none  [the longest x2 28.6 us: dispatch(): return lax.all_to_all(buffer, 'ep', split_axis=1, concat_axis=1, tiled=True)]
    reshape x2, local copies, waits for them, and re-layouts: 37.5 us -> 0.19 us  [the longest x1 0.11 us: body(): by_place = new_layout.reshape(2, 4, 4, 4)]
    all_to_all x3 -> x0, local copies, waits for them, and re-layouts: 25.3 us -> none  [the longest x1 16.2 us: dispatch(): return lax.all_to_all(buffer, 'ep', split_axis=1, concat_axis=1, tiled=True)]
  transfers between devices with their start and end apart: 9 -> 0, of which waited for: 7 -> 0; matrix products, arithmetic and copies ran while one was open for 15% -> 0% of each run, Pallas kernels for 0% -> 0%
where the time goes in v1:
time: 402 us; the launch traced here: 397 us
  Pallas kernels  377 us (94%)
  local copies, waits for them, and re-layouts  14.8 us (4%)
  other arithmetic  4.21 us (1%)
    pallas_call x1, Pallas kernels, give_back(): pl.pallas_call(return_kernel, name='give_back', out_shape=(jax.ShapeDtype...  178 us
    pallas_call x1, Pallas kernels, dispatch(): pl.pallas_call(dispatch_kernel, name='dispatch', out_shape=(jax.ShapeDtyp...  145 us
    pallas_call x1, Pallas kernels, experts(): pl.pallas_call(expert_kernel, name='experts', grid=(2,), out_shape=(jax.S...  53.8 us

profile of v1, /device:TPU:0, one launch (start us, length us, event | category | flops | bytes accessed | tf_op | source)
XLA Modules:
  0.0 396.9 jit_solution(6185247086079468720)
XLA Ops:
  0.7 1.2 dynamic_slice.16
  1.9 1.6 gather_fusion
  3.5 0.8 select_reduce_fusion
  4.3 0.7 reduce_precision.9
  5.1 0.1 reshape.199
  5.2 0.1 reshape.200
  5.3 0.1 convert_element_type.28
  5.4 0.1 dynamic_slice.18
  5.5 1.3 pad_add_fusion.facts
  6.8 0.7 broadcast_in_dim.35.e_cot
  7.4 0.7 broadcast_in_dim.34.e_tok
  8.1 0.1 copy.28
  8.2 0.8 copy.27
  9.0 0.8 copy.29
  9.8 1.9 concatenate.14.cot_ref
  11.7 1.9 concatenate.13.tok_ref
  13.6 1.3 fusion.perm
  14.8 145.0 %dispatch.1 = (bf16[2,8,96,2176]{3,2,1,0:T(8,128)(2,1)}, bf16[2,8,96,2048]{3,2,1,0:T(8,128)(2,1)}, bf16[8,1024,192]{2,1,0:T(8,128)(2,1)}, bf16[8,1024,192]{2,1,0...) custom-call(bf16[128,2176]{1,0:T(8,128)(2,1)} %concatenate.13.tok_ref, ...), custom_call_target="tpu_custom_call" | custom-call | tf_op jit(solution)/shard_map/dispatch/pallas_call | solution.py:203
  159.8 53.8 %experts.1 = (bf16[2,768,2176]{2,1,0:T(8,128)(2,1)}, bf16[2,768,2048]{2,1,0:T(8,128)(2,1)}, bf16[2,2048,384]{2,1,0:T(8,128)(2,1)}, bf16[2,2048,384]{2,1,0:T(8,128)(2,1)}, bf16[2,384,2048]{2,1,0:T(8,128)(2,1)}) custom-call(s32[3]{0:T(128)} %pad_add_fusion.facts, bf16[2,768,2176]{2,1,0:T(8,128)(2,1)} %bitcast.6, bf16[2,768,2048]{2,1,0:T(8,128)(2,1)} %bitcast.8, ...), custom_call_target="tpu_custom_call" | custom-call | tf_op jit(solution)/shard_map/experts/pallas_call | solution.py:333
  213.7 178.4 %give_back.1 = (bf16[128,1024]{1,0:T(8,128)(2,1)}, bf16[128,1024]{1,0:T(8,128)(2,1)}, f32[128,8]{1,0:T(8,128)}) custom-call(bf16[2,8,96,2176]{3,2,1,0:T(8,128)(2,1)} %bitcast.7, bf16[2,8,96,2048]{3,2,1,0:T(8,128)(2,1)} %bitcast.9, bf16[8,1024,192]{2,1,0:T(8,128)(2,1)} %get-tuple-element.28.st_tok, bf16[8,1024,192]{2,1,0:T(8,128)(2,1)} %get-tuple-element.29.st_cot), custom_call_target="tpu_custom_call" | custom-call | tf_op jit(solution)/shard_map/give_back/pallas_call | solution.py:485
  392.1 1.5 copy.31
  393.6 1.7 copy.34
  395.3 1.7 copy.35
  (10 shorter events, 0.1 us)

commit v2 on v1

--- a/solution.py
+++ b/solution.py
@@ -11,9 +11,12 @@
 META = 128
 WIDE = D + META
 BLOCKS = 8
+GROUP, SPAN = 4 * CAP, 4 * TOK
 ROWS = BLOCKS * CAP
 ALL = BLOCKS * ROWS
 HALF = D // 2
+Q = 4
+PART = HALF // Q
 LIMIT = 66 * 1024 * 1024 - 4096
 EP = ("xlo", "z", "y", "c")
 ANY = pl.BlockSpec(memory_space=pl.ANY)
@@ -99,10 +102,10 @@
     for copy in weights:
         copy.start()
 
-    row = lax.broadcasted_iota(jnp.int32, (ROWS, BLOCKS * TOK), 0)
-    col = lax.broadcasted_iota(jnp.int32, (ROWS, BLOCKS * TOK), 1)
-    value = jnp.full((ROWS, BLOCKS * TOK), -2, jnp.int32)
-    for b in range(BLOCKS):
+    row = lax.broadcasted_iota(jnp.int32, (GROUP, SPAN), 0)
+    col = lax.broadcasted_iota(jnp.int32, (GROUP, SPAN), 1)
+    value = jnp.full((GROUP, SPAN), -2, jnp.int32)
+    for b in range(4):
         inside = (row >= b * CAP) & (row < (b + 1) * CAP) & (col >= b * TOK) & (col < (b + 1) * TOK)
         value = jnp.where(inside, row - b * CAP, value)
     rowcode[...] = value.astype(F32)
@@ -119,7 +122,7 @@
             come[i].wait_recv()
         local.wait()
 
-    for gathered, experts, code in ((g_tok, e_tok, code_tok), (g_cot, e_cot, code_cot)):
+    def choose(gathered, experts, code, st):
         for b in range(BLOCKS):
             ids = gathered[b, :, D:WIDE].astype(F32).T[0:TOP]
             member = jnp.zeros((16, TOK), F32)
@@ -130,30 +133,38 @@
             for d in range(8):
                 code[d, 0:2, b * TOK : (b + 1) * TOK] = found[2 * d : 2 * d + 2]
 
-    def emit(d, gathered, code, sel, st, width):
-        rows = code[d]
-        chosen = jnp.concatenate(
-            [jnp.where(rowcode[...] == rows[l : l + 1], 1.0, 0.0) for l in range(2)], axis=0
-        )
-        st[d] = chosen.T.astype(BF)
-        pick = chosen.astype(BF)
+        def fill(d, carry):
+            rows = code[d]
+            for g in range(2):
+                for l in range(2):
+                    wanted = rows[l : l + 1, g * SPAN : (g + 1) * SPAN]
+                    to = pl.ds(pl.multiple_of(d * 2 * GROUP + l * GROUP, GROUP), GROUP)
+                    st[g, to] = jnp.where(rowcode[...] == wanted, 1.0, 0.0).astype(BF)
+            return carry
+
+        lax.fori_loop(0, 8, fill, 0)
+
+    def emit(pair, gathered, sel, st, width):
+        from_rows = pl.ds(pl.multiple_of(pair * 4 * GROUP, 4 * GROUP), 4 * GROUP)
 
         def piece(start, size):
-            source = gathered[:, :, pl.ds(start, size)].reshape(BLOCKS * TOK, size)
-            got = jnp.dot(pick, source, preferred_element_type=F32).astype(BF)
-            sel[d, :, :, pl.ds(start, size)] = got.reshape(2, ROWS, size)
+            cols = pl.ds(start, size)
+            for g in range(2):
+                source = gathered[g * 4 : (g + 1) * 4, :, cols].reshape(SPAN, size)
+                got = jnp.dot(st[g, from_rows], source, preferred_element_type=F32).astype(BF)
+                sel[pl.ds(pair * 2, 2), :, g * GROUP : (g + 1) * GROUP, cols] = got.reshape(2, 2, GROUP, size)
 
         def step(n, carry):
-            piece(pl.multiple_of(n * 256, 256), 256)
+            piece(pl.multiple_of(n * 512, 512), 512)
             return carry
 
-        lax.fori_loop(0, D // 256, step, 0)
+        lax.fori_loop(0, D // 512, step, 0)
         if width > D:
             piece(D, META)
 
     sides = (
-        (0, g_tok, code_tok, sel_tok, st_tok, st_tok_out, x_out, "z", me_z, WIDE),
-        (1, g_cot, code_cot, sel_cot, st_cot, st_cot_out, dy_out, "y", me_y, D),
+        (0, g_tok, e_tok, code_tok, sel_tok, st_tok, st_tok_out, x_out, "z", z, WIDE),
+        (1, g_cot, e_cot, code_cot, sel_cot, st_cot, st_cot_out, dy_out, "y", y, D),
     )
 
     def exchange(p, j, sel, target, axis, slot):
@@ -162,32 +173,35 @@
             {axis: j // 2, "c": lax.rem(j, 2)},
         )
 
+    for p, gathered, experts, code, sel, st, st_out, target, axis, b, width in sides:
+        choose(gathered, experts, code, st)
+        pltpu.make_async_copy(st, st_out, st_sem.at[p]).start()
+
     def send(i, carry):
-        for p, gathered, code, sel, st, st_out, target, axis, me, width in sides:
-            d = lax.rem(me + i, 8)
-            emit(d, gathered, code, sel, st, width)
-            exchange(p, d, sel, target, axis, me).start()
-            pltpu.make_async_copy(st.at[d], st_out.at[d], st_sem.at[p, d]).start()
-        return carry
-
-    lax.fori_loop(1, 8, send, 0)
-    for p, gathered, code, sel, st, st_out, target, axis, me, width in sides:
-        emit(me, gathered, code, sel, st, width)
-        pltpu.make_async_copy(sel.at[me], target.at[:, me], loc_sem.at[2 + p]).start()
-        pltpu.make_async_copy(st.at[me], st_out.at[me], st_sem.at[p, me]).start()
+        for p, gathered, experts, code, sel, st, st_out, target, axis, b, width in sides:
+            pair = lax.rem(b + i, 4)
+            emit(pair, gathered, sel, st, width)
+            for core in range(2):
+                exchange(p, pair * 2 + core, sel, target, axis, b * 2 + c).start()
+        return carry
+
+    lax.fori_loop(1, 4, send, 0)
+    for p, gathered, experts, code, sel, st, st_out, target, axis, b, width in sides:
+        emit(b, gathered, sel, st, width)
+        exchange(p, b * 2 + 1 - c, sel, target, axis, b * 2 + c).start()
+        pltpu.make_async_copy(sel.at[b * 2 + c], target.at[:, b * 2 + c], loc_sem.at[2 + p]).start()
 
     def finish(i, carry):
-        for p, gathered, code, sel, st, st_out, target, axis, me, width in sides:
-            j = lax.rem(me + i, 8)
+        for p, gathered, experts, code, sel, st, st_out, target, axis, b, width in sides:
+            j = lax.rem(b * 2 + c + i, 8)
             exchange(p, j, sel, target, axis, j).wait_send()
             exchange(p, j, sel, target, axis, j).wait_recv()
-            pltpu.make_async_copy(st.at[j], st_out.at[j], st_sem.at[p, j]).wait()
         return carry
 
     lax.fori_loop(1, 8, finish, 0)
-    for p, gathered, code, sel, st, st_out, target, axis, me, width in sides:
-        pltpu.make_async_copy(sel.at[me], target.at[:, me], loc_sem.at[2 + p]).wait()
-        pltpu.make_async_copy(st.at[me], st_out.at[me], st_sem.at[p, me]).wait()
+    for p, gathered, experts, code, sel, st, st_out, target, axis, b, width in sides:
+        pltpu.make_async_copy(sel.at[b * 2 + c], target.at[:, b * 2 + c], loc_sem.at[2 + p]).wait()
+        pltpu.make_async_copy(st, st_out, st_sem.at[p]).wait()
     for out, _, _ in (tok, cot):
         for copy in out:
             copy.wait_send()
@@ -197,7 +211,7 @@
 
 def dispatch(tok, cot, e_tok, e_cot, wg, wu, wd):
     gathered = pltpu.VMEM((BLOCKS, TOK, WIDE), BF)
-    choice = pltpu.VMEM((8, BLOCKS * TOK, 2 * ROWS), BF)
+    choice = pltpu.VMEM((2, ALL, SPAN), BF)
     code = pltpu.VMEM((8, 8, BLOCKS * TOK), F32)
     dma = pltpu.SemaphoreType.DMA
     return pl.pallas_call(
@@ -206,8 +220,8 @@
         out_shape=(
             jax.ShapeDtypeStruct((2, 8, ROWS, WIDE), BF),
             jax.ShapeDtypeStruct((2, 8, ROWS, D), BF),
-            jax.ShapeDtypeStruct((8, BLOCKS * TOK, 2 * ROWS), BF),
-            jax.ShapeDtypeStruct((8, BLOCKS * TOK, 2 * ROWS), BF),
+            jax.ShapeDtypeStruct((2, ALL, SPAN), BF),
+            jax.ShapeDtypeStruct((2, ALL, SPAN), BF),
             jax.ShapeDtypeStruct((D, FF), BF),
             jax.ShapeDtypeStruct((D, FF), BF),
             jax.ShapeDtypeStruct((FF, D), BF),
@@ -218,8 +232,8 @@
             gathered, gathered,
             pltpu.VMEM((8, 2, ROWS, WIDE), BF), pltpu.VMEM((8, 2, ROWS, D), BF),
             choice, choice, code, code,
-            pltpu.VMEM((ROWS, BLOCKS * TOK), F32), pltpu.VMEM((TOK, TOK), BF),
-            dma((2, 9)), dma((2, 9)), dma((2, 8)), dma((2, 8)), dma((2, 8)), dma((4,)), dma((3,)), dma((3,)),
+            pltpu.VMEM((GROUP, SPAN), F32), pltpu.VMEM((TOK, TOK), BF),
+            dma((2, 9)), dma((2, 9)), dma((2, 8)), dma((2, 8)), dma((2,)), dma((4,)), dma((3,)), dma((3,)),
         ],
         compiler_params=pltpu.CompilerParams(
             collective_id=0, has_side_effects=True, vmem_limit_bytes=LIMIT
@@ -229,7 +243,7 @@
 
 def expert_kernel(
     facts, x, dy, perm, wg, wu, wd, wg_new, wu_new, wd_new,
-    y, dx, gg, gu, gd,
+    y, ym, dx, gg, gu, gd,
     vg, vu, vd, gate, upper, dh_hi, dh_lo, hid, dgate, dup, hid_c, dgate_c, dup_c, sem,
 ):
     l = pl.program_id(0)
@@ -292,7 +306,7 @@
         )
         w = jnp.sum(named * weight, axis=1, keepdims=True)
         dc = jnp.sum(hidden * dh, axis=1, keepdims=True)
-        y[0, rows, D:WIDE] = (named * dc).astype(BF)
+        ym[0, rows] = (named * dc).astype(BF)
         hid[rows] = (hidden * w).astype(BF)
         dh = dh * w
         dgate[rows] = (dh * u * sigma * (1.0 + g * (1.0 - sigma))).astype(BF)
@@ -301,14 +315,20 @@
 
     lax.fori_loop(0, ALL // 192, second, 0)
 
+    def store(ref, rows, value):
+        for q in range(Q):
+            for t in range(2):
+                start = t * HALF + q * PART
+                ref[q, 0, rows, t * PART : (t + 1) * PART] = value[:, start : start + PART]
+
     def third(i, carry):
         rows = pl.ds(pl.multiple_of(i * 192, 192), 192)
         order = perm[rows]
-        y[0, rows, 0:D] = nn(hid[rows], vd[l]).astype(BF)
+        store(y, rows, nn(hid[rows], vd[l]).astype(BF))
         a = nn(order, dgate[...]).astype(BF)
         b = nn(order, dup[...]).astype(BF)
         hid_c[rows] = nn(order, hid[...]).astype(BF)
-        dx[0, rows] = (nt(a, vg[l]) + nt(b, vu[l])).astype(BF)
+        store(dx, rows, (nt(a, vg[l]) + nt(b, vu[l])).astype(BF))
         return carry
 
     lax.fori_loop(0, ALL // 192, third, 0)
@@ -328,6 +348,7 @@
     def block(*shape):
         return pl.BlockSpec((1, *shape), lambda l: (l,) + (0,) * len(shape))
 
+    parts = pl.BlockSpec((Q, 1, ALL, 2 * PART), lambda l: (0, l, 0, 0))
     small = pltpu.VMEM((ALL, FF), BF)
     wide = pltpu.VMEM((ALL, FF), F32)
     return pl.pallas_call(
@@ -335,8 +356,9 @@
         name="experts",
         grid=(2,),
         out_shape=(
-            jax.ShapeDtypeStruct((2, ALL, WIDE), BF),
-            jax.ShapeDtypeStruct((2, ALL, D), BF),
+            jax.ShapeDtypeStruct((Q, 2, ALL, 2 * PART), BF),
+            jax.ShapeDtypeStruct((2, ALL, META), BF),
+            jax.ShapeDtypeStruct((Q, 2, ALL, 2 * PART), BF),
             jax.ShapeDtypeStruct((2, D, FF), BF),
             jax.ShapeDtypeStruct((2, D, FF), BF),
             jax.ShapeDtypeStruct((2, FF, D), BF),
@@ -347,7 +369,7 @@
             pl.BlockSpec((ALL, ALL), lambda l: (0, 0), pipeline_mode=pl.Buffered(1)),
             ANY, ANY, ANY, ANY, ANY, ANY,
         ],
-        out_specs=[block(ALL, WIDE), block(ALL, D), block(D, FF), block(D, FF), block(FF, D)],
+        out_specs=[parts, block(ALL, META), parts, block(D, FF), block(D, FF), block(FF, D)],
         scratch_shapes=[
             pltpu.VMEM((2, D, FF), BF), pltpu.VMEM((2, D, FF), BF), pltpu.VMEM((2, FF, D), BF),
             wide, wide, small, small, small, small, small, small, small, small,
@@ -360,128 +382,183 @@
 
 
 def return_kernel(
-    y_ref, dx_ref, st_tok, st_cot,
+    y_ref, ym_ref, dx_ref, st_tok, st_cot,
     mixed, d_tokens, d_combine,
-    c_tok, c_cot, s_tok, s_cot, m_tok, m_cot, rx_tok, rx_cot, xs_tok, xs_cot, ra_tok, ra_cot,
-    a_send, a_recv, x_send, x_recv, f_send, f_recv, loc_sem,
+    c_tok, c_meta, c_cot, raw_tok, raw_cot, s_tok, s_cot, m_tok, m_meta, m_cot,
+    h_tok, h_meta, h_cot, rx_tok, rx_meta, rx_cot, xs_tok, xs_meta, xs_cot, ra_tok, ra_meta, ra_cot,
+    a_send, a_recv, h_send, h_recv, x_send, x_recv, f_send, f_recv, loc_sem, st_sem,
 ):
     at = position()
     xlo, y, z, c, xhi = at["xlo"], at["y"], at["z"], at["c"], at["xhi"]
-    me_z, me_y = z * 2 + c, y * 2 + c
-    flips = ((0, 1), (1, 0), (1, 1))
-    near = []
-    for fx, ft in flips:
-        near.append((1 - xlo if fx else xlo, 1 - xhi if ft else xhi))
-    greet([{"xlo": a, "xhi": b} for a, b in near] + others("z", me_z) + others("y", me_y))
-
-    sides = (
-        (0, y_ref, c_tok, st_tok, s_tok, m_tok, rx_tok, xs_tok, ra_tok, "z", me_z, "y", y, HALF + META),
-        (1, dx_ref, c_cot, st_cot, s_cot, m_cot, rx_cot, xs_cot, ra_cot, "y", me_y, "z", z, HALF),
-    )
-
-    def exchange(p, source, held, axis, j, slot):
+    near = ({"xlo": 1 - xlo}, {"xlo": 1 - xlo, "xhi": 1 - xhi})
+    their_t = (xhi, 1 - xhi)
+    greet([*near, *others("z", z * 2 + c), *others("y", y * 2 + c)])
+
+    tok = (0, y_ref, c_tok, s_tok, m_tok, h_tok, rx_tok, xs_tok, ra_tok, "z", z * 2 + c, "y", y)
+    cot = (1, dx_ref, c_cot, s_cot, m_cot, h_cot, rx_cot, xs_cot, ra_cot, "y", y * 2 + c, "z", z)
+    small = (2, ym_ref, c_meta, s_tok, m_meta, h_meta, rx_meta, xs_meta, ra_meta, "z", z * 2 + c, "y", y)
+
+    def exchange(side, q, j, slot):
+        p, source, held, s, m, h, rx, xs, ra, axis, me, other, a = side
         return remote(
-            source.at[:, j], held.at[slot], a_send.at[p, j], a_recv.at[p, slot],
+            source.at[q, :, j], held.at[q, slot], a_send.at[p, q, j], a_recv.at[p, q, slot],
             {axis: j // 2, "c": lax.rem(j, 2)},
         )
 
-    def send(i, carry):
-        for p, source, held, st, s, m, rx, xs, ra, axis, me, other, a, width in sides:
-            exchange(p, source, held, axis, lax.rem(me + i, 8), me).start()
-        return carry
-
-    lax.fori_loop(1, 8, send, 0)
-    for p, source, held, st, s, m, rx, xs, ra, axis, me, other, a, width in sides:
-        pltpu.make_async_copy(source.at[:, me], held.at[me], loc_sem.at[p]).start()
-        pltpu.make_async_copy(st, s, loc_sem.at[2 + p]).start()
-
-    def spread(p, m, rx, k):
-        a, b = near[k]
-        return remote(m.at[a, b], rx.at[xlo * 2 + xhi], x_send.at[p, k], x_recv.at[p, k], {"xlo": a, "xhi": b})
-
-    for p, source, held, st, s, m, rx, xs, ra, axis, me, other, a, width in sides:
+    def own(side, q):
+        p, source, held, s, m, h, rx, xs, ra, axis, me, other, a = side
+        return pltpu.make_async_copy(source.at[q, :, me], held.at[q, me], loc_sem.at[p, q])
+
+    def relay(side, q, k):
+        p, source, held, s, m, h, rx, xs, ra, axis, me, other, a = side
+        piece = m.at[q, xlo, 0 if p == 2 else 1 - xhi, pl.ds(2 * k, 2)]
+        return remote(piece, h.at[q, k], h_send.at[p, q, k], h_recv.at[p, q, k], near[k])
+
+    def spread(side, q, k):
+        p, source, held, s, m, h, rx, xs, ra, axis, me, other, a = side
+        piece = m.at[q, 1 - xlo, k if p == 2 else their_t[k]]
+        return remote(piece, rx.at[q, k], x_send.at[p, q, k], x_recv.at[p, q, k], near[k])
+
+    def fold(side, q, k, slot):
+        p, source, held, s, m, h, rx, xs, ra, axis, me, other, a = side
+        to = lax.rem(a + k, 4)
+        return remote(xs.at[q, to], ra.at[q, slot], f_send.at[p, q, k], f_recv.at[p, q, k], {other: to})
+
+    def begin(side, q):
+        def send(i, carry):
+            exchange(side, q, lax.rem(side[10] + i, 8), side[10]).start()
+            return carry
+
+        lax.fori_loop(1, 8, send, 0)
+        own(side, q).start()
+
+    def begin_part(q, carry):
+        begin(tok, q)
+        begin(cot, q)
+        return carry
+
+    begin(small, 0)
+    lax.fori_loop(0, Q, begin_part, 0)
+    loads = [
+        pltpu.make_async_copy(src, raw, st_sem.at[i]) for i, (src, raw) in enumerate(((st_tok, raw_tok), (st_cot, raw_cot)))
+    ]
+    for load in loads:
+        load.start()
+    for load, raw, s in ((loads[0], raw_tok, s_tok), (loads[1], raw_cot, s_cot)):
+        load.wait()
+        for g in range(2):
+
+            def turn(n, carry, raw=raw, s=s, g=g):
+                cols = pl.ds(pl.multiple_of(n * 128, 128), 128)
+                s[g, cols] = raw[g, :, cols].astype(F32).T.astype(BF)
+                return carry
+
+            lax.fori_loop(0, SPAN // 128, turn, 0)
+
+    def combine(side, q):
+        p, source, held, s, m, h, rx, xs, ra, axis, me, other, a = side
 
         def arrive(i, carry):
-            exchange(p, source, held, axis, lax.rem(me + i, 8), lax.rem(me + i, 8)).wait_recv()
+            j = lax.rem(me + i, 8)
+            exchange(side, q, j, j).wait_recv()
             return carry
 
         lax.fori_loop(1, 8, arrive, 0)
-        pltpu.make_async_copy(source.at[:, me], held.at[me], loc_sem.at[p]).wait()
-        pltpu.make_async_copy(st, s, loc_sem.at[2 + p]).wait()
-
-        def total(start, size):
-            acc = jnp.zeros((BLOCKS * TOK, size), F32)
-            for d in range(8):
-                part = held[d, :, :, pl.ds(start, size)].reshape(2 * ROWS, size)
-                acc = acc + jnp.dot(s[d], part, preferred_element_type=F32)
-            return acc.astype(BF).reshape(2, 4, TOK, size)
-
-        for t in range(2):
-
-            def step(n, carry):
-                got = total(pl.multiple_of(t * HALF + n * 256, 256), 256)
-                cols = pl.ds(pl.multiple_of(n * 256, 256), 256)
-                for b in range(2):
-                    m[b, t, :, :, cols] = got[b]
-                return carry
-
-            lax.fori_loop(0, HALF // 256, step, 0)
-        if width > HALF:
-            got = total(D, META)
-            for t in range(2):
-                for b in range(2):
-                    m[b, t, :, :, HALF:width] = got[b]
-        for k in range(3):
-            spread(p, m, rx, k).start()
-
-    def fold(p, xs, ra, other, a, k, slot):
-        to = lax.rem(a + k, 4)
-        return remote(xs.at[to], ra.at[slot], f_send.at[p, k], f_recv.at[p, k], {other: to})
-
-    for p, source, held, st, s, m, rx, xs, ra, axis, me, other, a, width in sides:
-        for k in range(3):
-            spread(p, m, rx, k).wait_recv()
-
-        def add(i, carry):
-            acc = m[xlo, xhi, i].astype(F32)
-            for k in range(3):
-                acc = acc + rx[near[k][0] * 2 + near[k][1], i].astype(F32)
-            xs[i] = acc.astype(BF)
+        own(side, q).wait()
+        size = held.shape[-1]
+        for g in range(2):
+            part = held[q, :, :, g * GROUP : (g + 1) * GROUP].reshape(ALL, size)
+            got = jnp.dot(s[g], part, preferred_element_type=F32).astype(BF)
+            if p == 2:
+                for t in range(2):
+                    m[q, g, t] = got.reshape(4, TOK, META)
+            else:
+                for t in range(2):
+                    m[q, g, t] = got[:, t * PART : (t + 1) * PART].reshape(4, TOK, PART)
+        for k in range(2):
+            relay(side, q, k).start()
+
+    def pass_on(side, q):
+        p, source, held, s, m, h, rx, xs, ra, axis, me, other, a = side
+        for k in range(2):
+            relay(side, q, k).wait_recv()
+            t = (1 - k) if p == 2 else their_t[1 - k]
+            half = pl.ds(2 * k, 2)
+            total = m[q, 1 - xlo, t, half].astype(F32) + h[q, k].astype(F32)
+            m[q, 1 - xlo, t, half] = total.astype(BF)
+        for k in range(2):
+            spread(side, q, k).start()
+
+    def gather(side, q):
+        p, source, held, s, m, h, rx, xs, ra, axis, me, other, a = side
+        for k in range(2):
+            spread(side, q, k).wait_recv()
+        total = m[q, xlo, 0 if p == 2 else xhi].astype(F32)
+        for k in range(2):
+            total = total + rx[q, k].astype(F32)
+        xs[q] = total.astype(BF)
+        for k in range(1, 4):
+            fold(side, q, k, a).start()
+
+    def close(side, q):
+        p, source, held, s, m, h, rx, xs, ra, axis, me, other, a = side
+        for k in range(1, 4):
+            fold(side, q, k, a).wait_recv()
+        total = xs[q, a].astype(F32)
+        for k in range(1, 4):
+            total = total + ra[q, lax.rem(a + k, 4)].astype(F32)
+        if p == 2:
+            d_combine[...] = total[:, 0:TOP]
+        else:
+            (mixed, d_tokens)[p][:, pl.ds(pl.multiple_of(q * PART, PART), PART)] = total.astype(BF)
+        for k in range(2):
+            relay(side, q, k).wait_send()
+            spread(side, q, k).wait_send()
+            fold(side, q, k + 1, a).wait_send()
+        fold(side, q, 3, a).wait_send()
+
+        def sent(i, carry):
+            exchange(side, q, lax.rem(me + i, 8), me).wait_send()
             return carry
 
-        lax.fori_loop(0, 4, add, 0)
-        for k in range(1, 4):
-            fold(p, xs, ra, other, a, k, a).start()
-
-    for p, source, held, st, s, m, rx, xs, ra, axis, me, other, a, width in sides:
-        for k in range(1, 4):
-            fold(p, xs, ra, other, a, k, a).wait_recv()
-        acc = xs[a].astype(F32)
-        for k in range(1, 4):
-            acc = acc + ra[lax.rem(a + k, 4)].astype(F32)
-        (mixed, d_tokens)[p][...] = acc[:, 0:HALF].astype(BF)
-        if width > HALF:
-            d_combine[...] = acc[:, HALF : HALF + TOP]
-    for p, source, held, st, s, m, rx, xs, ra, axis, me, other, a, width in sides:
-
-        def sent(i, carry):
-            exchange(p, source, held, axis, lax.rem(me + i, 8), me).wait_send()
-            return carry
-
         lax.fori_loop(1, 8, sent, 0)
-        for k in range(3):
-            spread(p, m, rx, k).wait_send()
-            fold(p, xs, ra, other, a, k + 1, a).wait_send()
-
-
-def give_back(y, dx, st_tok, st_cot):
+
+    def both(stage, q):
+        stage(tok, q)
+        stage(cot, q)
+
+    combine(small, 0)
+    both(combine, 0)
+    pass_on(small, 0)
+    both(pass_on, 0)
+    both(combine, 1)
+    gather(small, 0)
+    both(gather, 0)
+    both(pass_on, 1)
+
+    def flow(q, carry):
+        both(combine, q)
+        both(gather, q - 1)
+        both(pass_on, q)
+        both(close, q - 2)
+        return carry
+
+    lax.fori_loop(2, Q, flow, 0)
+    close(small, 0)
+    both(gather, Q - 1)
+    both(close, Q - 2)
+    both(close, Q - 1)
+
+
+def give_back(y, ym, dx, st_tok, st_cot):
     dma = pltpu.SemaphoreType.DMA
-    choice = pltpu.VMEM((8, BLOCKS * TOK, 2 * ROWS), BF)
-    wide = HALF + META
-
-    def both(*shape):
-        return [pltpu.VMEM((*shape, wide), BF), pltpu.VMEM((*shape, HALF), BF)]
-
+
+    def each(*shape):
+        return [
+            pltpu.VMEM((Q, *shape, PART), BF), pltpu.VMEM((1, *shape, META), BF), pltpu.VMEM((Q, *shape, PART), BF)
+        ]
+
+    held = (8, 2, ROWS)
     return pl.pallas_call(
         return_kernel,
         name="give_back",
@@ -490,18 +567,20 @@
             jax.ShapeDtypeStruct((TOK, HALF), BF),
             jax.ShapeDtypeStruct((TOK, TOP), F32),
         ),
-        in_specs=[ANY] * 4,
+        in_specs=[ANY] * 5,
         out_specs=[VMEM] * 3,
         scratch_shapes=[
-            pltpu.VMEM((8, 2, ROWS, WIDE), BF), pltpu.VMEM((8, 2, ROWS, D), BF),
-            choice, choice,
-            *both(2, 2, 4, TOK), *both(4, 4, TOK), *both(4, TOK), *both(4, TOK),
-            dma((2, 8)), dma((2, 8)), dma((2, 3)), dma((2, 3)), dma((2, 4)), dma((2, 4)), dma((4,)),
+            pltpu.VMEM((Q, *held, 2 * PART), BF), pltpu.VMEM((1, *held, META), BF), pltpu.VMEM((Q, *held, 2 * PART), BF),
+            pltpu.VMEM((2, ALL, SPAN), BF), pltpu.VMEM((2, ALL, SPAN), BF),
+            pltpu.VMEM((2, SPAN, ALL), BF), pltpu.VMEM((2, SPAN, ALL), BF),
+            *each(2, 2, 4, TOK), *each(2, 2, TOK), *each(2, 4, TOK), *each(4, TOK), *each(4, TOK),
+            dma((3, Q, 8)), dma((3, Q, 8)), dma((3, Q, 2)), dma((3, Q, 2)), dma((3, Q, 2)), dma((3, Q, 2)),
+            dma((3, Q, 4)), dma((3, Q, 4)), dma((3, Q)), dma((2,)),
         ],
         compiler_params=pltpu.CompilerParams(
             collective_id=1, has_side_effects=True, vmem_limit_bytes=LIMIT
         ),
-    )(y, dx, st_tok, st_cot)
+    )(y, ym, dx, st_tok, st_cot)
 
 
 def body(tokens, expert_ids, combine, cotangent, old_layout, pair_moves, gate_w, up_w, down_w):
@@ -537,12 +616,13 @@
     r = jnp.arange(ALL, dtype=jnp.int32)
     there = (r // CAP % 4 * 2 + r // ROWS % 2) * ROWS + (r // (4 * CAP) % 2 * 4 + r // (2 * ROWS)) * CAP + r % CAP
     perm = (there[:, None] == r[None, :]).astype(BF)
-    y_rows, dx_rows, gg, gu, gd = experts(
+    y_rows, y_meta, dx_rows, gg, gu, gd = experts(
         facts, x.reshape(2, ALL, WIDE), dy.reshape(2, ALL, D), perm,
         gate_w, up_w, down_w, wg_new, wu_new, wd_new,
     )
     mixed, d_tokens, d_combine = give_back(
-        y_rows.reshape(2, 8, ROWS, WIDE), dx_rows.reshape(2, 8, ROWS, D), st_tok, st_cot
+        y_rows.reshape(Q, 2, 8, ROWS, 2 * PART), y_meta.reshape(1, 2, 8, ROWS, META),
+        dx_rows.reshape(Q, 2, 8, ROWS, 2 * PART), st_tok, st_cot,
     )
     return mixed, d_tokens, d_combine, gg, gu, gd
 

time: 402 us -> 322 us (0.80); the launches traced: 397 us -> 322 us
  Pallas kernels: 377 us -> 302 us
    pallas_call x1, Pallas kernels: 178 us -> 110 us  [give_back(): pl.pallas_call(return_kernel, name='give_back', out_shape=(jax.ShapeDtype...]
    pallas_call x1, Pallas kernels: 145 us -> 138 us  [dispatch(): pl.pallas_call(dispatch_kernel, name='dispatch', out_shape=(jax.ShapeDtyp...]
where the time goes in v2:
time: 322 us
  Pallas kernels  302 us (94%)
  local copies, waits for them, and re-layouts  14.8 us (5%)
  other arithmetic  4.24 us (1%)
    pallas_call x1, Pallas kernels, dispatch(): pl.pallas_call(dispatch_kernel, name='dispatch', out_shape=(jax.ShapeDtyp...  138 us
    pallas_call x1, Pallas kernels, give_back(): pl.pallas_call(return_kernel, name='give_back', out_shape=(jax.ShapeDtype...  110 us
    pallas_call x1, Pallas kernels, experts(): pl.pallas_call(expert_kernel, name='experts', grid=(2,), out_shape=(jax.S...  53.9 us

profile of v2, /device:TPU:0, one launch (start us, length us, event | category | flops | bytes accessed | tf_op | source)
XLA Modules:
  0.0 321.8 jit_solution(14496811266380472623)
XLA Ops:
  0.7 1.2 dynamic_slice.16
  1.9 1.6 gather_fusion
  3.5 0.8 select_reduce_fusion
  4.3 0.7 reduce_precision.9
  5.1 0.1 reshape.202
  5.2 0.1 reshape.203
  5.3 0.1 convert_element_type.28
  5.4 0.1 dynamic_slice.18
  5.5 1.3 pad_add_fusion.facts
  6.8 0.7 broadcast_in_dim.35.e_cot
  7.5 0.7 broadcast_in_dim.34.e_tok
  8.1 0.1 copy.28
  8.2 0.8 copy.27
  9.0 0.8 copy.29
  9.9 1.9 concatenate.14.cot_ref
  11.7 1.9 concatenate.13.tok_ref
  13.6 1.3 fusion.perm
  14.9 137.6 %dispatch.1 = (bf16[2,8,96,2176]{3,2,1,0:T(8,128)(2,1)}, bf16[2,8,96,2048]{3,2,1,0:T(8,128)(2,1)}, bf16[2,768,512]{2,1,0:T(8,128)(2,1)}, bf16[2,768,512]{2,1,0:T...) custom-call(bf16[128,2176]{1,0:T(8,128)(2,1)} %concatenate.13.tok_ref, ...), custom_call_target="tpu_custom_call" | custom-call | tf_op jit(solution)/shard_map/dispatch/pallas_call | solution.py:217
  152.5 53.9 %experts.1 = (bf16[4,2,768,512]{3,2,1,0:T(8,128)(2,1)}, bf16[2,768,128]{2,1,0:T(8,128)(2,1)}, bf16[4,2,768,512]{3,2,1,0:T(8,128)(2,1)}, bf16[2,2048,384]{2,1,0:T...) custom-call(s32[3]{0:T(128)} %pad_add_fusion.facts, bf16[2,768,2176]{2,1,0:T(8,128)(2,1)} %bitcast.7, ...), custom_call_target="tpu_custom_call" | custom-call | tf_op jit(solution)/shard_map/experts/pallas_call | solution.py:354
  206.4 110.5 %give_back.1 = (bf16[128,1024]{1,0:T(8,128)(2,1)}, bf16[128,1024]{1,0:T(8,128)(2,1)}, f32[128,8]{1,0:T(8,128)}) custom-call(bf16[4,2,8,96,512]{4,3,2,1,0:T(8,128)(2,1)} %bitcast.8, bf16[1,2,8,96,128]{4,3,2,1,0:T(8,128)(2,1)} %bitcast.11, bf16[4,2,8,96,512]{4,3,2,1,0:T(8,128)(2,1)} %bitcast.9, bf16[2,768,512]{2,1,0:T(8,128)(2,1)} %get-tuple-element.30.st_tok, ...), custom_call_target="tpu_custom_call" | custom-call | tf_op jit(solution)/shard_map/give_back/pallas_call | solution.py:562
  316.9 1.5 copy.31
  318.4 1.7 copy.34
  320.1 1.7 copy.35
  (10 shorter events, 0.1 us)

commit v3 on v2

--- a/solution.py
+++ b/solution.py
@@ -9,7 +9,7 @@
 BF, F32 = jnp.bfloat16, jnp.float32
 D, FF, CAP, TOK, TOP = 2048, 384, 12, 128, 8
 META = 128
-WIDE = D + META
+WIDE = META + D
 BLOCKS = 8
 GROUP, SPAN = 4 * CAP, 4 * TOK
 ROWS = BLOCKS * CAP
@@ -53,48 +53,95 @@
     return found
 
 
+def expert_at(old_layout, pair_moves, device, l):
+    if l == 0:
+        return old_layout[device * 2]
+    source = jnp.where(pair_moves[device] == 1, lax.rem(device + 32, 64), device)
+    return old_layout[source * 2 + 1]
+
+
 def dispatch_kernel(
-    tok_ref, cot_ref, e_tok, e_cot, wg, wu, wd,
-    x_out, dy_out, st_tok_out, st_cot_out, wg_out, wu_out, wd_out,
-    g_tok, g_cot, sel_tok, sel_cot, st_tok, st_cot, code_tok, code_cot, rowcode, upper,
-    ag_send, ag_recv, x_send, x_recv, st_sem, loc_sem, w_send, w_recv,
+    tok_ref, cot_ref, ids_ref, combine_ref, old_layout, pair_moves, wg, wu, wd,
+    x_out, dy_out, st_tok_out, st_cot_out, wg_out, wu_out, wd_out, perm_out,
+    g0_tok, g1_tok, g0_cot, g1_cot, sel0_tok, sel1_tok, sel0_cot, sel1_cot,
+    st_tok, st_cot, code_tok, code_cot, e_tok, e_cot, rowcode, upper, perm,
+    ag_send, ag_recv, x_send, x_recv, st_sem, in_sem, loc_sem, w_send, w_recv,
 ):
     at = position()
     xlo, y, z, c, xhi = at["xlo"], at["y"], at["z"], at["c"], at["xhi"]
     direct, flipped = {"xlo": 1 - xlo}, {"xlo": 1 - xlo, "xhi": 1 - xhi}
     me_z, me_y = z * 2 + c, y * 2 + c
+
+    gathers = (
+        (0, tok_ref, (g0_tok, g1_tok), "y", y),
+        (1, cot_ref, (g0_cot, g1_cot), "z", z),
+    )
+
+    def load(side, h):
+        p, source, gathered, axis, a = side
+        target = gathered[h].at[xlo * 4 + a]
+        if h == 0:
+            target = target.at[:, META : META + HALF]
+        return pltpu.make_async_copy(source.at[:, h * HALF : (h + 1) * HALF], target, in_sem.at[p, h])
+
+    for h in range(2):
+        for side in gathers:
+            load(side, h).start()
+    w = combine_ref[...]
+    high = w.astype(BF).astype(F32)
+    middle = (w - high).astype(BF).astype(F32)
+    facts = jnp.concatenate(
+        [ids_ref[...].astype(F32), high, middle, w - high - middle, jnp.zeros((META - 32, TOK), F32)], axis=0
+    )
+    meta = facts.T.astype(BF)
+    for p, source, gathered, axis, a in gathers:
+        gathered[0][xlo * 4 + a, :, 0:META] = meta
     greet([direct, flipped] + others("z", me_z) + others("y", me_y))
 
-    paths = ((tok_ref, g_tok, "y", y, 0), (cot_ref, g_cot, "z", z, 1))
-
-    def copies(source, gathered, axis, a, p):
+    def copies(side, h):
+        p, source, gathered, axis, a = side
+        held = gathered[h]
         right, left = {axis: lax.rem(a + 1, 4)}, {axis: lax.rem(a + 3, 4)}
         opposite = lax.rem(a + 2, 4)
         mine, theirs = xlo * 4, (1 - xlo) * 4
         l, r = lax.rem(a + 3, 4), lax.rem(a + 1, 4)
         lo, hi = pl.ds(0, 64), pl.ds(64, 64)
-        own = gathered.at[mine + a]
+        own = held.at[mine + a]
         plan = [
-            (source, own, flipped, gathered.at[theirs + a]),
-            (source, own, right, gathered.at[mine + l]),
-            (source, own, left, gathered.at[mine + r]),
-            (gathered.at[theirs + a], gathered.at[theirs + a], right, gathered.at[theirs + l]),
-            (gathered.at[theirs + a], gathered.at[theirs + a], left, gathered.at[theirs + r]),
-            (gathered.at[mine + l, lo], gathered.at[mine + l, lo], right, gathered.at[mine + opposite, lo]),
-            (gathered.at[theirs + l, lo], gathered.at[theirs + l, lo], right, gathered.at[theirs + opposite, lo]),
-            (gathered.at[mine + r, hi], gathered.at[mine + r, hi], left, gathered.at[mine + opposite, hi]),
-            (gathered.at[theirs + r, hi], gathered.at[theirs + r, hi], left, gathered.at[theirs + opposite, hi]),
+            (own, flipped, held.at[theirs + a]),
+            (own, right, held.at[mine + l]),
+            (own, left, held.at[mine + r]),
+            (held.at[theirs + a], right, held.at[theirs + l]),
+            (held.at[theirs + a], left, held.at[theirs + r]),
+            (held.at[mine + l, lo], right, held.at[mine + opposite, lo]),
+            (held.at[theirs + l, lo], right, held.at[theirs + opposite, lo]),
+            (held.at[mine + r, hi], left, held.at[mine + opposite, hi]),
+            (held.at[theirs + r, hi], left, held.at[theirs + opposite, hi]),
         ]
-        out = [remote(s, t, ag_send.at[p, i], ag_recv.at[p, i], dev) for i, (s, t, dev, _) in enumerate(plan)]
-        come = [remote(s, got, ag_send.at[p, i], ag_recv.at[p, i], dev) for i, (s, _, dev, got) in enumerate(plan)]
-        local = pltpu.make_async_copy(source, own, loc_sem.at[p])
-        return out, come, local
-
-    tok, cot = copies(*paths[0]), copies(*paths[1])
-    for out, _, local in (tok, cot):
-        for i in (1, 2, 0):
-            out[i].start()
-        local.start()
+        out = [remote(t, t, ag_send.at[p, h, i], ag_recv.at[p, h, i], dev) for i, (t, dev, _) in enumerate(plan)]
+        come = [remote(t, got, ag_send.at[p, h, i], ag_recv.at[p, h, i], dev) for i, (t, dev, got) in enumerate(plan)]
+        return out, come
+
+    moves = [[copies(side, h) for side in gathers] for h in range(2)]
+
+    def open_half(h):
+        for side, (out, _) in zip(gathers, moves[h]):
+            load(side, h).wait()
+            for i in (1, 2, 0):
+                out[i].start()
+
+    def pass_half(h, arrival, starts):
+        for out, come in moves[h]:
+            come[arrival].wait_recv()
+            for i in starts:
+                out[i].start()
+
+    def close_half(h):
+        for out, come in moves[h]:
+            for i in (5, 6, 7, 8):
+                come[i].wait_recv()
+
+    open_half(0)
     weights = [
         remote(src.at[1], dst, w_send.at[i], w_recv.at[i], direct)
         for i, (src, dst) in enumerate(((wg, wg_out), (wu, wu_out), (wd, wd_out)))
@@ -111,20 +158,40 @@
     rowcode[...] = value.astype(F32)
     before = lax.broadcasted_iota(jnp.int32, (TOK, TOK), 0) < lax.broadcasted_iota(jnp.int32, (TOK, TOK), 1)
     upper[...] = jnp.where(before, 1.0, 0.0).astype(BF)
-
-    for arrival, starts in ((0, (3, 4)), (1, (5,)), (2, (7,)), (3, (6,)), (4, (8,))):
-        for out, come, _ in (tok, cot):
-            come[arrival].wait_recv()
-            for i in starts:
-                out[i].start()
-    for out, come, local in (tok, cot):
-        for i in (5, 6, 7, 8):
-            come[i].wait_recv()
-        local.wait()
+    place = lax.broadcasted_iota(jnp.int32, (16, TOK), 0)
+    along_z, along_y = jnp.zeros((16, TOK), jnp.int32), jnp.zeros((16, TOK), jnp.int32)
+    for slot in range(16):
+        b, core, l = slot // 4, slot // 2 % 2, slot % 2
+        found = expert_at(old_layout, pair_moves, ((xlo * 4 + b) * 4 + y) * 2 + core, l)
+        along_z = jnp.where(place == slot, found, along_z)
+        found = expert_at(old_layout, pair_moves, ((xlo * 4 + z) * 4 + b) * 2 + core, l)
+        along_y = jnp.where(place == slot, found, along_y)
+    e_tok[...] = along_z.astype(F32)
+    e_cot[...] = along_y.astype(F32)
+
+    pass_half(0, 0, (3, 4))
+    pass_half(0, 1, (5,))
+    pass_half(0, 2, (7,))
+    open_half(1)
+
+    def strip(i, carry):
+        lr = lax.broadcasted_iota(jnp.int32, (GROUP, ALL), 0)
+        lc = lax.broadcasted_iota(jnp.int32, (GROUP, ALL), 1)
+        inner = jnp.where(lr >= 12, 1, 0) + jnp.where(lr >= 24, 1, 0) + jnp.where(lr >= 36, 1, 0)
+        there = i * GROUP + lr + (2 * ROWS - CAP) * (inner - i // 4)
+        perm[pl.ds(pl.multiple_of(i * GROUP, GROUP), GROUP)] = jnp.where(lc == there, 1.0, 0.0).astype(BF)
+        return carry
+
+    lax.fori_loop(0, ALL // GROUP, strip, 0)
+    perm_copy = pltpu.make_async_copy(perm, perm_out, loc_sem.at[4])
+    perm_copy.start()
+    pass_half(0, 3, (6,))
+    pass_half(0, 4, (8,))
+    close_half(0)
 
     def choose(gathered, experts, code, st):
         for b in range(BLOCKS):
-            ids = gathered[b, :, D:WIDE].astype(F32).T[0:TOP]
+            ids = gathered[b, :, 0:META].astype(F32).T[0:TOP]
             member = jnp.zeros((16, TOK), F32)
             for k in range(TOP):
                 member = member + jnp.where(ids[k : k + 1] == experts[...], 1.0, 0.0)
@@ -144,76 +211,94 @@
 
         lax.fori_loop(0, 8, fill, 0)
 
-    def emit(pair, gathered, sel, st, width):
+    def emit(pair, gathered, start, sel, st):
+        width = sel.shape[-1]
         from_rows = pl.ds(pl.multiple_of(pair * 4 * GROUP, 4 * GROUP), 4 * GROUP)
-
-        def piece(start, size):
-            cols = pl.ds(start, size)
-            for g in range(2):
-                source = gathered[g * 4 : (g + 1) * 4, :, cols].reshape(SPAN, size)
-                got = jnp.dot(st[g, from_rows], source, preferred_element_type=F32).astype(BF)
-                sel[pl.ds(pair * 2, 2), :, g * GROUP : (g + 1) * GROUP, cols] = got.reshape(2, 2, GROUP, size)
-
-        def step(n, carry):
-            piece(pl.multiple_of(n * 512, 512), 512)
-            return carry
-
-        lax.fori_loop(0, D // 512, step, 0)
-        if width > D:
-            piece(D, META)
+        for g in range(2):
+            source = gathered[g * 4 : (g + 1) * 4, :, start : start + width].reshape(SPAN, width)
+            got = jnp.dot(st[g, from_rows], source, preferred_element_type=F32).astype(BF)
+            sel[pl.ds(pair * 2, 2), :, g * GROUP : (g + 1) * GROUP] = got.reshape(2, 2, GROUP, width)
 
     sides = (
-        (0, g_tok, e_tok, code_tok, sel_tok, st_tok, st_tok_out, x_out, "z", z, WIDE),
-        (1, g_cot, e_cot, code_cot, sel_cot, st_cot, st_cot_out, dy_out, "y", y, D),
+        (0, (g0_tok, g1_tok), e_tok, code_tok, (sel0_tok, sel1_tok), st_tok, st_tok_out, x_out, "z", z, (0, META + HALF)),
+        (1, (g0_cot, g1_cot), e_cot, code_cot, (sel0_cot, sel1_cot), st_cot, st_cot_out, dy_out, "y", y, (0, HALF)),
     )
 
-    def exchange(p, j, sel, target, axis, slot):
+    def target(side, h, slot):
+        out, sel, start = side[7], side[4][h], side[10][h]
+        return out.at[:, slot, :, pl.ds(start, sel.shape[-1])]
+
+    def exchange(side, h, j, slot):
+        p, sel, axis = side[0], side[4][h], side[8]
         return remote(
-            sel.at[j], target.at[:, slot], x_send.at[p, j], x_recv.at[p, slot],
+            sel.at[j], target(side, h, slot), x_send.at[p, h, j], x_recv.at[p, h, slot],
             {axis: j // 2, "c": lax.rem(j, 2)},
         )
 
-    for p, gathered, experts, code, sel, st, st_out, target, axis, b, width in sides:
-        choose(gathered, experts, code, st)
+    def keep(side, h):
+        j = side[9] * 2 + c
+        return pltpu.make_async_copy(side[4][h].at[j], target(side, h, j), loc_sem.at[2 * side[0] + h])
+
+    def produce(h, i):
+        for side in sides:
+            p, gathered, experts, code, sel, st, st_out, out, axis, b, starts = side
+            pair = lax.rem(b + i, 4)
+            skip = META if h == 0 and p == 1 else 0
+            emit(pair, gathered[h], skip, sel[h], st)
+            if i < 4:
+                for core in range(2):
+                    exchange(side, h, pair * 2 + core, b * 2 + c).start()
+            else:
+                exchange(side, h, b * 2 + 1 - c, b * 2 + c).start()
+                keep(side, h).start()
+
+    for side in sides:
+        p, gathered, experts, code, sel, st, st_out, out, axis, b, starts = side
+        choose(gathered[0], experts, code, st)
         pltpu.make_async_copy(st, st_out, st_sem.at[p]).start()
-
-    def send(i, carry):
-        for p, gathered, experts, code, sel, st, st_out, target, axis, b, width in sides:
-            pair = lax.rem(b + i, 4)
-            emit(pair, gathered, sel, st, width)
-            for core in range(2):
-                exchange(p, pair * 2 + core, sel, target, axis, b * 2 + c).start()
-        return carry
-
-    lax.fori_loop(1, 4, send, 0)
-    for p, gathered, experts, code, sel, st, st_out, target, axis, b, width in sides:
-        emit(b, gathered, sel, st, width)
-        exchange(p, b * 2 + 1 - c, sel, target, axis, b * 2 + c).start()
-        pltpu.make_async_copy(sel.at[b * 2 + c], target.at[:, b * 2 + c], loc_sem.at[2 + p]).start()
-
-    def finish(i, carry):
-        for p, gathered, experts, code, sel, st, st_out, target, axis, b, width in sides:
-            j = lax.rem(b * 2 + c + i, 8)
-            exchange(p, j, sel, target, axis, j).wait_send()
-            exchange(p, j, sel, target, axis, j).wait_recv()
-        return carry
-
-    lax.fori_loop(1, 8, finish, 0)
-    for p, gathered, experts, code, sel, st, st_out, target, axis, b, width in sides:
-        pltpu.make_async_copy(sel.at[b * 2 + c], target.at[:, b * 2 + c], loc_sem.at[2 + p]).wait()
-        pltpu.make_async_copy(st, st_out, st_sem.at[p]).wait()
-    for out, _, _ in (tok, cot):
-        for copy in out:
-            copy.wait_send()
+        if p == 0:
+            pass_half(1, 0, (3, 4))
+    produce(0, 1)
+    pass_half(1, 1, (5,))
+    pass_half(1, 2, (7,))
+    produce(0, 2)
+    pass_half(1, 3, (6,))
+    pass_half(1, 4, (8,))
+    produce(0, 3)
+    produce(0, 4)
+    close_half(1)
+    for i in range(1, 5):
+        produce(1, i)
+
+    for h in range(2):
+
+        def finish(i, carry):
+            for side in sides:
+                j = lax.rem(side[9] * 2 + c + i, 8)
+                exchange(side, h, j, j).wait_send()
+                exchange(side, h, j, j).wait_recv()
+            return carry
+
+        lax.fori_loop(1, 8, finish, 0)
+        for side in sides:
+            keep(side, h).wait()
+        for out, _ in moves[h]:
+            for copy in out:
+                copy.wait_send()
+    for side in sides:
+        pltpu.make_async_copy(side[5], side[6], st_sem.at[side[0]]).wait()
+    perm_copy.wait()
     for copy in weights:
         copy.wait()
 
 
-def dispatch(tok, cot, e_tok, e_cot, wg, wu, wd):
-    gathered = pltpu.VMEM((BLOCKS, TOK, WIDE), BF)
+def dispatch(tok, cot, ids, combine, old_layout, pair_moves, wg, wu, wd):
     choice = pltpu.VMEM((2, ALL, SPAN), BF)
     code = pltpu.VMEM((8, 8, BLOCKS * TOK), F32)
     dma = pltpu.SemaphoreType.DMA
+    smem = pl.BlockSpec(memory_space=pltpu.SMEM)
+    halves = [pltpu.VMEM((BLOCKS, TOK, META + HALF), BF), pltpu.VMEM((BLOCKS, TOK, HALF), BF)]
+    wide, narrow = pltpu.VMEM((8, 2, ROWS, META + HALF), BF), pltpu.VMEM((8, 2, ROWS, HALF), BF)
     return pl.pallas_call(
         dispatch_kernel,
         name="dispatch",
@@ -225,29 +310,32 @@
             jax.ShapeDtypeStruct((D, FF), BF),
             jax.ShapeDtypeStruct((D, FF), BF),
             jax.ShapeDtypeStruct((FF, D), BF),
+            jax.ShapeDtypeStruct((ALL, ALL), BF),
         ),
-        in_specs=[ANY, ANY, VMEM, VMEM, ANY, ANY, ANY],
-        out_specs=[ANY] * 7,
+        in_specs=[ANY, ANY, VMEM, VMEM, smem, smem, ANY, ANY, ANY],
+        out_specs=[ANY] * 8,
         scratch_shapes=[
-            gathered, gathered,
-            pltpu.VMEM((8, 2, ROWS, WIDE), BF), pltpu.VMEM((8, 2, ROWS, D), BF),
-            choice, choice, code, code,
-            pltpu.VMEM((GROUP, SPAN), F32), pltpu.VMEM((TOK, TOK), BF),
-            dma((2, 9)), dma((2, 9)), dma((2, 8)), dma((2, 8)), dma((2,)), dma((4,)), dma((3,)), dma((3,)),
+            *halves, *halves, wide, narrow, narrow, narrow,
+            choice, choice, code, code, pltpu.VMEM((16, TOK), F32), pltpu.VMEM((16, TOK), F32),
+            pltpu.VMEM((GROUP, SPAN), F32), pltpu.VMEM((TOK, TOK), BF), pltpu.VMEM((ALL, ALL), BF),
+            dma((2, 2, 9)), dma((2, 2, 9)), dma((2, 2, 8)), dma((2, 2, 8)), dma((2,)), dma((2, 2)), dma((5,)),
+            dma((3,)), dma((3,)),
         ],
         compiler_params=pltpu.CompilerParams(
             collective_id=0, has_side_effects=True, vmem_limit_bytes=LIMIT
         ),
-    )(tok, cot, e_tok, e_cot, wg, wu, wd)
+    )(tok, cot, ids, combine, old_layout, pair_moves, wg, wu, wd)
 
 
 def expert_kernel(
-    facts, x, dy, perm, wg, wu, wd, wg_new, wu_new, wd_new,
+    old_layout, pair_moves, x, dy, perm, wg, wu, wd, wg_new, wu_new, wd_new,
     y, ym, dx, gg, gu, gd,
     vg, vu, vd, gate, upper, dh_hi, dh_lo, hid, dgate, dup, hid_c, dgate_c, dup_c, sem,
 ):
     l = pl.program_id(0)
-    moved = facts[0] == 1
+    at = position()
+    device = ((at["xlo"] * 4 + at["z"]) * 4 + at["y"]) * 2 + at["c"]
+    moved = pair_moves[device] == 1
     pairs = ((wg, wg_new, vg), (wu, wu_new, vu), (wd, wd_new, vd))
 
     @pl.when(l == 0)
@@ -266,7 +354,9 @@
 
     for i, (old, new, held) in enumerate(pairs):
         pltpu.make_async_copy(old.at[0], held.at[l], sem.at[l, i]).wait()
-    expert = jnp.where(l == 0, facts[1], facts[2]).astype(F32)
+    expert = jnp.where(
+        l == 0, expert_at(old_layout, pair_moves, device, 0), expert_at(old_layout, pair_moves, device, 1)
+    ).astype(F32)
 
     def nt(a, b):
         return lax.dot_general(a, b, (((1,), (1,)), ((), ())), preferred_element_type=F32)
@@ -279,7 +369,7 @@
 
     def first(i, carry):
         rows = pl.ds(pl.multiple_of(i * 384, 384), 384)
-        own = x[0, rows, 0:D]
+        own = x[0, rows, META:WIDE]
         gate[rows] = nn(own, vg[l])
         upper[rows] = nn(own, vu[l])
         dh = nt(dy[0, rows], vd[l])
@@ -298,7 +388,7 @@
         sigma = jax.nn.sigmoid(g)
         active = g * sigma
         hidden = active * u
-        meta = x[0, rows, D:WIDE].astype(F32)
+        meta = x[0, rows, 0:META].astype(F32)
         lane = lax.broadcasted_iota(jnp.int32, meta.shape, 1)
         named = jnp.where((meta == expert) & (lane < TOP), 1.0, 0.0)
         weight = pltpu.roll(meta, META - 8, 1) + (
@@ -335,7 +425,7 @@
 
     def fourth(i, carry):
         cols = pl.ds(pl.multiple_of(i * 512, 512), 512)
-        own = x[0, :, cols]
+        own = x[0, :, pl.ds(pl.multiple_of(META + i * 512, 128), 512)]
         gg[0, cols] = tn(own, dgate[...]).astype(BF)
         gu[0, cols] = tn(own, dup[...]).astype(BF)
         gd[0, :, cols] = tn(hid_c[...], dy[0, :, cols]).astype(BF)
@@ -344,7 +434,7 @@
     lax.fori_loop(0, D // 512, fourth, 0)
 
 
-def experts(facts, x, dy, perm, wg, wu, wd, wg_new, wu_new, wd_new):
+def experts(old_layout, pair_moves, x, dy, perm, wg, wu, wd, wg_new, wu_new, wd_new):
     def block(*shape):
         return pl.BlockSpec((1, *shape), lambda l: (l,) + (0,) * len(shape))
 
@@ -364,7 +454,7 @@
             jax.ShapeDtypeStruct((2, FF, D), BF),
         ),
         in_specs=[
-            pl.BlockSpec(memory_space=pltpu.SMEM),
+            pl.BlockSpec(memory_space=pltpu.SMEM), pl.BlockSpec(memory_space=pltpu.SMEM),
             block(ALL, WIDE), block(ALL, D),
             pl.BlockSpec((ALL, ALL), lambda l: (0, 0), pipeline_mode=pl.Buffered(1)),
             ANY, ANY, ANY, ANY, ANY, ANY,
@@ -378,7 +468,7 @@
         compiler_params=pltpu.CompilerParams(
             dimension_semantics=("arbitrary",), vmem_limit_bytes=LIMIT
         ),
-    )(facts, x, dy, perm, wg, wu, wd, wg_new, wu_new, wd_new)
+    )(old_layout, pair_moves, x, dy, perm, wg, wu, wd, wg_new, wu_new, wd_new)
 
 
 def return_kernel(
@@ -508,7 +598,7 @@
         for k in range(1, 4):
             total = total + ra[q, lax.rem(a + k, 4)].astype(F32)
         if p == 2:
-            d_combine[...] = total[:, 0:TOP]
+            d_combine[...] = total.T[0:TOP]
         else:
             (mixed, d_tokens)[p][:, pl.ds(pl.multiple_of(q * PART, PART), PART)] = total.astype(BF)
         for k in range(2):
@@ -565,7 +655,7 @@
         out_shape=(
             jax.ShapeDtypeStruct((TOK, HALF), BF),
             jax.ShapeDtypeStruct((TOK, HALF), BF),
-            jax.ShapeDtypeStruct((TOK, TOP), F32),
+            jax.ShapeDtypeStruct((TOP, TOK), F32),
         ),
         in_specs=[ANY] * 5,
         out_specs=[VMEM] * 3,
@@ -584,47 +674,18 @@
 
 
 def body(tokens, expert_ids, combine, cotangent, old_layout, pair_moves, gate_w, up_w, down_w):
-    at = position()
-    xlo, y, z, c = at["xlo"], at["y"], at["z"], at["c"]
-    slots = jnp.arange(128, dtype=jnp.int32)
-    owner, local = slots // 2, slots % 2
-    moved = (local == 1) & (pair_moves[owner] == 1)
-    source = jnp.where(moved, (owner + 32) % 64 * 2 + local, slots)
-    new_layout = jnp.sum(jnp.where(source[:, None] == slots[None, :], old_layout[None, :], 0), axis=1)
-    by_place = new_layout.reshape(2, 4, 4, 4)
-    plane = lax.dynamic_index_in_dim(by_place, xlo, 0, False)
-    at_y = lax.dynamic_index_in_dim(plane, y, 1, False)
-    at_z = lax.dynamic_index_in_dim(plane, z, 0, False)
-    own = lax.dynamic_slice(at_z.reshape(16), ((y * 2 + c) * 2,), (2,))
-    device = ((xlo * 4 + z) * 4 + y) * 2 + c
-    flag = lax.dynamic_slice(pair_moves, (device,), (1,))
-    facts = jnp.concatenate([flag, own])
-    e_tok = jnp.broadcast_to(at_y.reshape(16, 1), (16, TOK)).astype(F32)
-    e_cot = jnp.broadcast_to(at_z.reshape(16, 1), (16, TOK)).astype(F32)
-
-    high = lax.reduce_precision(combine, 8, 7)
-    middle = lax.reduce_precision(combine - high, 8, 7)
-    low = lax.reduce_precision(combine - high - middle, 8, 7)
-    meta = jnp.concatenate(
-        [expert_ids.astype(BF), high.astype(BF), middle.astype(BF), low.astype(BF), jnp.zeros((TOK, META - 32), BF)],
-        axis=1,
+    x, dy, st_tok, st_cot, wg_new, wu_new, wd_new, perm = dispatch(
+        tokens, cotangent, expert_ids.T, combine.T, old_layout, pair_moves, gate_w, up_w, down_w
     )
-    tok = jnp.concatenate([tokens, meta], axis=1)
-    cot = jnp.concatenate([cotangent, meta], axis=1)
-    x, dy, st_tok, st_cot, wg_new, wu_new, wd_new = dispatch(tok, cot, e_tok, e_cot, gate_w, up_w, down_w)
-
-    r = jnp.arange(ALL, dtype=jnp.int32)
-    there = (r // CAP % 4 * 2 + r // ROWS % 2) * ROWS + (r // (4 * CAP) % 2 * 4 + r // (2 * ROWS)) * CAP + r % CAP
-    perm = (there[:, None] == r[None, :]).astype(BF)
     y_rows, y_meta, dx_rows, gg, gu, gd = experts(
-        facts, x.reshape(2, ALL, WIDE), dy.reshape(2, ALL, D), perm,
+        old_layout, pair_moves, x.reshape(2, ALL, WIDE), dy.reshape(2, ALL, D), perm,
         gate_w, up_w, down_w, wg_new, wu_new, wd_new,
     )
     mixed, d_tokens, d_combine = give_back(
         y_rows.reshape(Q, 2, 8, ROWS, 2 * PART), y_meta.reshape(1, 2, 8, ROWS, META),
         dx_rows.reshape(Q, 2, 8, ROWS, 2 * PART), st_tok, st_cot,
     )
-    return mixed, d_tokens, d_combine, gg, gu, gd
+    return mixed, d_tokens, d_combine.T, gg, gu, gd
 
 
 def solution(mesh):

time: 322 us -> 300 us (0.932)
  local copies, waits for them, and re-layouts: 14.8 us -> 4.61 us
  Pallas kernels: 302 us -> 294 us
  other arithmetic: 4.24 us -> 0 us
    pallas_call x1, Pallas kernels: 138 us -> 129 us  [dispatch(): pl.pallas_call(dispatch_kernel, name='dispatch', out_shape=(jax.ShapeDtyp...]
    concatenate x2 -> x0, local copies, waits for them, and re-layouts: 3.73 us -> none  [the longest x1 1.87 us: body(): cot = jnp.concatenate([cotangent, meta], axis=1)]
where the time goes in v3:
time: 300 us
  Pallas kernels  294 us (98%)
  local copies, waits for them, and re-layouts  4.61 us (2%)
    pallas_call x1, Pallas kernels, dispatch(): pl.pallas_call(dispatch_kernel, name='dispatch', out_shape=(jax.ShapeDtyp...  129 us
    pallas_call x1, Pallas kernels, give_back(): pl.pallas_call(return_kernel, name='give_back', out_shape=(jax.ShapeDtype...  111 us
    pallas_call x1, Pallas kernels, experts(): pl.pallas_call(expert_kernel, name='experts', grid=(2,), out_shape=(jax.S...  54.2 us

profile of v3, /device:TPU:0, one launch (start us, length us, event | category | flops | bytes accessed | tf_op | source)
XLA Modules:
  0.0 299.7 jit_solution(14447222310504092001)
XLA Ops:
  0.6 129.1 %dispatch.1 = (bf16[2,8,96,2176]{3,2,1,0:T(8,128)(2,1)}, bf16[2,8,96,2048]{3,2,1,0:T(8,128)(2,1)}, bf16[2,768,512]{2,1,0:T(8,128)(2,1)}, bf16[2,768,512]{2,1,0:T...) custom-call(bf16[128,2048]{1,0:T(8,128)(2,1)} %tok_ref.1, ...), custom_call_target="tpu_custom_call" | custom-call | tf_op jit(solution)/shard_map/dispatch/pallas_call | solution.py:302
  129.8 54.2 %experts.1 = (bf16[4,2,768,512]{3,2,1,0:T(8,128)(2,1)}, bf16[2,768,128]{2,1,0:T(8,128)(2,1)}, bf16[4,2,768,512]{3,2,1,0:T(8,128)(2,1)}, bf16[2,2048,384]{2,1,0:T...) custom-call(s32[128]{0:T(128)} %old_layout.3, s32[64]{0:T(128)} %pair_moves.3, ...), custom_call_target="tpu_custom_call" | custom-call | tf_op jit(solution)/shard_map/experts/pallas_call | solution.py:444
  183.9 111.1 %give_back.1 = (bf16[128,1024]{1,0:T(8,128)(2,1)}, bf16[128,1024]{1,0:T(8,128)(2,1)}, f32[8,128]{1,0:T(8,128)}) custom-call(bf16[4,2,8,96,512]{4,3,2,1,0:T(8,128)(2,1)} %bitcast.9, bf16[1,2,8,96,128]{4,3,2,1,0:T(8,128)(2,1)} %bitcast.12, bf16[4,2,8,96,512]{4,3,2,1,0:T(8,128)(2,1)} %bitcast.10, bf16[2,768,512]{2,1,0:T(8,128)(2,1)} %get-tuple-element.32.st_tok, ...), custom_call_target="tpu_custom_call" | custom-call | tf_op jit(solution)/shard_map/give_back/pallas_call | solution.py:652
  295.1 1.7 copy.18
  296.8 1.7 copy.19
  298.4 1.3 copy.20

commit v4 on v3

--- a/solution.py
+++ b/solution.py
@@ -330,7 +330,7 @@
 def expert_kernel(
     old_layout, pair_moves, x, dy, perm, wg, wu, wd, wg_new, wu_new, wd_new,
     y, ym, dx, gg, gu, gd,
-    vg, vu, vd, gate, upper, dh_hi, dh_lo, hid, dgate, dup, hid_c, dgate_c, dup_c, sem,
+    y_v, dx_v, vg, vu, vd, gate, upper, dh_hi, dh_lo, hid, dgate, dup, hid_c, dgate_c, dup_c, sem, out_sem,
 ):
     l = pl.program_id(0)
     at = position()
@@ -381,7 +381,7 @@
     lax.fori_loop(0, ALL // 384, first, 0)
 
     def second(i, carry):
-        rows = pl.ds(pl.multiple_of(i * 192, 192), 192)
+        rows = pl.ds(pl.multiple_of(i * 384, 384), 384)
         order = perm[rows]
         dh = nn(order, dh_hi[...]) + nn(order, dh_lo[...])
         g, u = gate[rows], upper[rows]
@@ -403,42 +403,49 @@
         dup[rows] = (dh * active).astype(BF)
         return carry
 
-    lax.fori_loop(0, ALL // 192, second, 0)
+    lax.fori_loop(0, ALL // 384, second, 0)
 
     def store(ref, rows, value):
         for q in range(Q):
             for t in range(2):
                 start = t * HALF + q * PART
-                ref[q, 0, rows, t * PART : (t + 1) * PART] = value[:, start : start + PART]
+                ref[q, rows, t * PART : (t + 1) * PART] = value[:, start : start + PART]
 
     def third(i, carry):
-        rows = pl.ds(pl.multiple_of(i * 192, 192), 192)
+        rows = pl.ds(pl.multiple_of(i * 384, 384), 384)
         order = perm[rows]
-        store(y, rows, nn(hid[rows], vd[l]).astype(BF))
+        store(y_v, rows, nn(hid[rows], vd[l]).astype(BF))
         a = nn(order, dgate[...]).astype(BF)
         b = nn(order, dup[...]).astype(BF)
         hid_c[rows] = nn(order, hid[...]).astype(BF)
-        store(dx, rows, (nt(a, vg[l]) + nt(b, vu[l])).astype(BF))
+        store(dx_v, rows, (nt(a, vg[l]) + nt(b, vu[l])).astype(BF))
         return carry
 
-    lax.fori_loop(0, ALL // 192, third, 0)
+    lax.fori_loop(0, ALL // 384, third, 0)
+    leaving = [
+        pltpu.make_async_copy(held, out.at[:, l], out_sem.at[i]) for i, (held, out) in enumerate(((y_v, y), (dx_v, dx)))
+    ]
+    for copy in leaving:
+        copy.start()
 
     def fourth(i, carry):
-        cols = pl.ds(pl.multiple_of(i * 512, 512), 512)
-        own = x[0, :, pl.ds(pl.multiple_of(META + i * 512, 128), 512)]
+        cols = pl.ds(pl.multiple_of(i * 1024, 1024), 1024)
+        own = x[0, :, pl.ds(pl.multiple_of(META + i * 1024, 128), 1024)]
         gg[0, cols] = tn(own, dgate[...]).astype(BF)
         gu[0, cols] = tn(own, dup[...]).astype(BF)
         gd[0, :, cols] = tn(hid_c[...], dy[0, :, cols]).astype(BF)
         return carry
 
-    lax.fori_loop(0, D // 512, fourth, 0)
+    lax.fori_loop(0, D // 1024, fourth, 0)
+    for copy in leaving:
+        copy.wait()
 
 
 def experts(old_layout, pair_moves, x, dy, perm, wg, wu, wd, wg_new, wu_new, wd_new):
     def block(*shape):
         return pl.BlockSpec((1, *shape), lambda l: (l,) + (0,) * len(shape))
 
-    parts = pl.BlockSpec((Q, 1, ALL, 2 * PART), lambda l: (0, l, 0, 0))
+    parts = pltpu.VMEM((Q, ALL, 2 * PART), BF)
     small = pltpu.VMEM((ALL, FF), BF)
     wide = pltpu.VMEM((ALL, FF), F32)
     return pl.pallas_call(
@@ -459,11 +466,11 @@
             pl.BlockSpec((ALL, ALL), lambda l: (0, 0), pipeline_mode=pl.Buffered(1)),
             ANY, ANY, ANY, ANY, ANY, ANY,
         ],
-        out_specs=[parts, block(ALL, META), parts, block(D, FF), block(D, FF), block(FF, D)],
+        out_specs=[ANY, block(ALL, META), ANY, block(D, FF), block(D, FF), block(FF, D)],
         scratch_shapes=[
-            pltpu.VMEM((2, D, FF), BF), pltpu.VMEM((2, D, FF), BF), pltpu.VMEM((2, FF, D), BF),
+            parts, parts, pltpu.VMEM((2, D, FF), BF), pltpu.VMEM((2, D, FF), BF), pltpu.VMEM((2, FF, D), BF),
             wide, wide, small, small, small, small, small, small, small, small,
-            pltpu.SemaphoreType.DMA((2, 3)),
+            pltpu.SemaphoreType.DMA((2, 3)), pltpu.SemaphoreType.DMA((2,)),
         ],
         compiler_params=pltpu.CompilerParams(
             dimension_semantics=("arbitrary",), vmem_limit_bytes=LIMIT
@@ -673,6 +680,22 @@
     )(y, ym, dx, st_tok, st_cot)
 
 
+def hand_over_kernel(a, b, c, a_out, b_out, c_out):
+    a_out[...] = a[...]
+    b_out[...] = b[...]
+    c_out[...] = c[...]
+
+
+def hand_over(*values):
+    return pl.pallas_call(
+        hand_over_kernel,
+        name="hand_over",
+        out_shape=tuple(jax.ShapeDtypeStruct(v.shape, v.dtype) for v in values),
+        in_specs=[VMEM] * 3,
+        out_specs=[VMEM] * 3,
+    )(*values)
+
+
 def body(tokens, expert_ids, combine, cotangent, old_layout, pair_moves, gate_w, up_w, down_w):
     x, dy, st_tok, st_cot, wg_new, wu_new, wd_new, perm = dispatch(
         tokens, cotangent, expert_ids.T, combine.T, old_layout, pair_moves, gate_w, up_w, down_w
@@ -685,6 +708,7 @@
         y_rows.reshape(Q, 2, 8, ROWS, 2 * PART), y_meta.reshape(1, 2, 8, ROWS, META),
         dx_rows.reshape(Q, 2, 8, ROWS, 2 * PART), st_tok, st_cot,
     )
+    mixed, d_tokens, d_combine = hand_over(mixed, d_tokens, d_combine)
     return mixed, d_tokens, d_combine.T, gg, gu, gd
 
 

time: 300 us -> 291 us (0.970)
  local copies, waits for them, and re-layouts: 4.61 us -> 0 us
  Pallas kernels: 294 us -> 290 us
    pallas_call x1, Pallas kernels: 54.2 us -> 47.6 us  [experts(): pl.pallas_call(expert_kernel, name='experts', grid=(2,), out_shape=(jax.S...]
    unnamed x3 -> x0, local copies, waits for them, and re-layouts: 4.61 us -> none
where the time goes in v4:
time: 291 us; the launch traced here: 290 us
  Pallas kernels  290 us (100%)
    pallas_call x1, Pallas kernels, dispatch(): pl.pallas_call(dispatch_kernel, name='dispatch', out_shape=(jax.ShapeDtyp...  129 us
    pallas_call x1, Pallas kernels, give_back(): pl.pallas_call(return_kernel, name='give_back', out_shape=(jax.ShapeDtype...  111 us
    pallas_call x1, Pallas kernels, experts(): pl.pallas_call(expert_kernel, name='experts', grid=(2,), out_shape=(jax.S...  47.6 us

profile of v4, /device:TPU:0, one launch (start us, length us, event | category | flops | bytes accessed | tf_op | source)
XLA Modules:
  0.0 290.4 jit_solution(15823851683174169817)
XLA Ops:
  0.6 129.1 %dispatch.1 = (bf16[2,8,96,2176]{3,2,1,0:T(8,128)(2,1)}, bf16[2,8,96,2048]{3,2,1,0:T(8,128)(2,1)}, bf16[2,768,512]{2,1,0:T(8,128)(2,1)}, bf16[2,768,512]{2,1,0:T...) custom-call(bf16[128,2048]{1,0:T(8,128)(2,1)} %tok_ref.1, ...), custom_call_target="tpu_custom_call" | custom-call | tf_op jit(solution)/shard_map/dispatch/pallas_call | solution.py:302
  129.8 47.6 %experts.1 = (bf16[4,2,768,512]{3,2,1,0:T(8,128)(2,1)}, bf16[2,768,128]{2,1,0:T(8,128)(2,1)}, bf16[4,2,768,512]{3,2,1,0:T(8,128)(2,1)}, bf16[2,2048,384]{2,1,0:T...) custom-call(s32[128]{0:T(128)} %old_layout.3, s32[64]{0:T(128)} %pair_moves.3, ...), custom_call_target="tpu_custom_call" | custom-call | tf_op jit(solution)/shard_map/experts/pallas_call | solution.py:451
  177.4 111.1 %give_back.1 = (bf16[128,1024]{1,0:T(8,128)(2,1)}, bf16[128,1024]{1,0:T(8,128)(2,1)}, f32[8,128]{1,0:T(8,128)}) custom-call(bf16[4,2,8,96,512]{4,3,2,1,0:T(8,128)(2,1)} %bitcast.9, bf16[1,2,8,96,128]{4,3,2,1,0:T(8,128)(2,1)} %bitcast.12, bf16[4,2,8,96,512]{4,3,2,1,0:T(8,128)(2,1)} %bitcast.10, bf16[2,768,512]{2,1,0:T(8,128)(2,1)} %get-tuple-element.35.st_tok, ...), custom_call_target="tpu_custom_call" | custom-call | tf_op jit(solution)/shard_map/give_back/pallas_call | solution.py:659
  288.6 1.8 hand_over.1

commit v5 on v4

--- a/solution.py
+++ b/solution.py
@@ -412,7 +412,7 @@
                 ref[q, rows, t * PART : (t + 1) * PART] = value[:, start : start + PART]
 
     def third(i, carry):
-        rows = pl.ds(pl.multiple_of(i * 384, 384), 384)
+        rows = pl.ds(pl.multiple_of(i * 768, 768), 768)
         order = perm[rows]
         store(y_v, rows, nn(hid[rows], vd[l]).astype(BF))
         a = nn(order, dgate[...]).astype(BF)
@@ -421,7 +421,7 @@
         store(dx_v, rows, (nt(a, vg[l]) + nt(b, vu[l])).astype(BF))
         return carry
 
-    lax.fori_loop(0, ALL // 384, third, 0)
+    lax.fori_loop(0, ALL // 768, third, 0)
     leaving = [
         pltpu.make_async_copy(held, out.at[:, l], out_sem.at[i]) for i, (held, out) in enumerate(((y_v, y), (dx_v, dx)))
     ]

time: 291 us -> 290 us (level)
  no operation moved by 1% of the time
where the time goes in v5:
time: 290 us
  Pallas kernels  289 us (100%)
    pallas_call x1, Pallas kernels, dispatch(): pl.pallas_call(dispatch_kernel, name='dispatch', out_shape=(jax.ShapeDtyp...  129 us
    pallas_call x1, Pallas kernels, give_back(): pl.pallas_call(return_kernel, name='give_back', out_shape=(jax.ShapeDtype...  111 us
    pallas_call x1, Pallas kernels, experts(): pl.pallas_call(expert_kernel, name='experts', grid=(2,), out_shape=(jax.S...  47.3 us

profile of v5, /device:TPU:0, one launch (start us, length us, event | category | flops | bytes accessed | tf_op | source)
XLA Modules:
  0.0 290.1 jit_solution(15285278238084315022)
XLA Ops:
  0.6 129.1 %dispatch.1 = (bf16[2,8,96,2176]{3,2,1,0:T(8,128)(2,1)}, bf16[2,8,96,2048]{3,2,1,0:T(8,128)(2,1)}, bf16[2,768,512]{2,1,0:T(8,128)(2,1)}, bf16[2,768,512]{2,1,0:T...) custom-call(bf16[128,2048]{1,0:T(8,128)(2,1)} %tok_ref.1, ...), custom_call_target="tpu_custom_call" | custom-call | tf_op jit(solution)/shard_map/dispatch/pallas_call | solution.py:302
  129.8 47.3 %experts.1 = (bf16[4,2,768,512]{3,2,1,0:T(8,128)(2,1)}, bf16[2,768,128]{2,1,0:T(8,128)(2,1)}, bf16[4,2,768,512]{3,2,1,0:T(8,128)(2,1)}, bf16[2,2048,384]{2,1,0:T...) custom-call(s32[128]{0:T(128)} %old_layout.3, s32[64]{0:T(128)} %pair_moves.3, ...), custom_call_target="tpu_custom_call" | custom-call | tf_op jit(solution)/shard_map/experts/pallas_call | solution.py:451
  177.1 111.1 %give_back.1 = (bf16[128,1024]{1,0:T(8,128)(2,1)}, bf16[128,1024]{1,0:T(8,128)(2,1)}, f32[8,128]{1,0:T(8,128)}) custom-call(bf16[4,2,8,96,512]{4,3,2,1,0:T(8,128)(2,1)} %bitcast.9, bf16[1,2,8,96,128]{4,3,2,1,0:T(8,128)(2,1)} %bitcast.12, bf16[4,2,8,96,512]{4,3,2,1,0:T(8,128)(2,1)} %bitcast.10, bf16[2,768,512]{2,1,0:T(8,128)(2,1)} %get-tuple-element.35.st_tok, ...), custom_call_target="tpu_custom_call" | custom-call | tf_op jit(solution)/shard_map/give_back/pallas_call | solution.py:659
  288.2 1.8 hand_over.1
